TPU v7x, 32 devices: a whole 2x2x4 slice. The times are simulated.
32 devices in a mesh: member: 8 (over z, x), space: 4 (over y, core).
Axes of the slice: x: 2, y: 2, z: 4, core: 2. Of those that a mesh axis runs over, the one named last changes fastest.
Arguments:
- states: float32 [1024, 24576], P('member', 'space'), may hold values from -6 to 6
- obs_values: float32 [2, 2048], replicated, may hold values from -6 to 6
- obs_weights: float32 [2, 2048], replicated, may hold values from 0.2 to 2
- obs_cell: int32 [2, 4, 4], P(None, 'space'), may hold values from 0 to 47
- op_select: int32 [2, 4, 4], P(None, 'space'), may hold values from 0 to 7
- op_table: float32 [8, 128, 128], replicated, may hold values from -0.5 to 0.5
- loc_obs: int32 [2, 4, 48, 8], P(None, 'space', 'member'), may hold values from 0 to 11
- loc_tile: int32 [2, 4, 48, 8], P(None, 'space', 'member'), may hold values from 0 to 7
- loc_tiles: float32 [8, 128, 128], replicated, may hold values from 0 to 1
Outputs:
- analysis: float32 [1024, 24576], P('member', 'space')
All inputs are finite; a program needn't handle non-finite values.
Results may differ from a plain program's by a relative error of at most 0.00012.
Values sent between devices are 32-bit elements; how exact they have to be, the bound alone decides.
A program may use at most 128 MiB of HBM per device.

v0:
```python
import jax
import jax.numpy as jnp
from jax import lax
from jax.sharding import PartitionSpec as P

K = 1024
BLK = 128
CB_DEV = 6
OB = 4


def with_halo(cells, sides, width):
    for axis, dim in sides:
        count = lax.axis_size(axis)
        head = lax.slice_in_dim(cells, 0, width, axis=dim)
        tail = lax.slice_in_dim(cells, cells.shape[dim] - width, cells.shape[dim], axis=dim)
        cells = jnp.concatenate(
            [
                lax.ppermute(tail, axis, [(i, (i + 1) % count) for i in range(count)]),
                cells,
                lax.ppermute(head, axis, [((i + 1) % count, i) for i in range(count)]),
            ],
            axis=dim,
        )
    return cells


def window_values(flat_row):
    space_n = lax.axis_size("space")
    slab_index = lax.axis_index("space")
    by_slab = flat_row.reshape(space_n, OB * BLK)
    slab_pick = (slab_index - 1 + jnp.arange(3, dtype=jnp.int32)) % space_n
    return by_slab[slab_pick].reshape(3 * OB * BLK)


def window(observed):
    return with_halo(observed, (("space", 1),), OB * BLK)


def prepare(window_obs, obs_values, obs_weights, batch_no):
    obs_mean = jnp.mean(window_obs, axis=0)
    obs_anom = window_obs - obs_mean
    values = window_values(obs_values[batch_no])
    weights = window_values(obs_weights[batch_no])
    innov = weights * (values - obs_mean) - 0.5 * weights * obs_anom
    return (obs_anom, innov)


def observe_members(ensemble, obs_cell, op_select, op_table, batch_no):
    blocks = ensemble.reshape(ensemble.shape[0], ensemble.shape[1] // BLK, BLK)
    picked = blocks[:, obs_cell[batch_no, 0]]
    operators = op_table[op_select[batch_no, 0]]
    observed = jnp.einsum("koc,opc->kop", picked, operators, precision=lax.Precision.HIGHEST)
    observed = observed.reshape(ensemble.shape[0], OB * BLK)
    return lax.all_gather(observed, "member", axis=0, tiled=True)


def observe_owners(cells, obs_cell, op_select, op_table, batch_no):
    member_index = lax.axis_index("member")
    cell_index = obs_cell[batch_no, 0]
    owned = cell_index // CB_DEV == member_index
    local_idx = cell_index % CB_DEV
    blocks = cells.reshape(K, CB_DEV, BLK)
    picked = blocks[:, local_idx]
    operators = op_table[op_select[batch_no, 0]]
    observed = jnp.einsum("koc,opc->kop", picked, operators, precision=lax.Precision.HIGHEST)
    observed = observed * owned.astype(jnp.float32)[None, :, None]
    return lax.psum(observed.reshape(K, OB * BLK), "member")


def to_cells(ensemble):
    return lax.all_to_all(ensemble, "member", split_axis=1, concat_axis=0, tiled=True)


def to_members(cells):
    return lax.all_to_all(cells, "member", split_axis=0, concat_axis=1, tiled=True)


def update_cells(cells, obs_anom, innov, loc_obs, loc_tile, loc_tiles, batch_no):
    blocks = cells.reshape(K, CB_DEV, BLK)
    state_mean = jnp.mean(blocks, axis=0)
    anom_win = obs_anom.reshape(K, 3 * OB, BLK)
    innov_win = innov.reshape(K, 3 * OB, BLK)

    def update_block(packed):
        cell_blk, mean_blk, reach, tile_pick = packed
        state_anom = cell_blk - mean_blk
        chosen = anom_win[:, reach]
        covariance = jnp.einsum(
            "kc,klo->lco", state_anom, chosen, precision=lax.Precision.HIGHEST
        ) / (K - 1)
        gain = loc_tiles[tile_pick] * covariance
        increment = jnp.einsum(
            "klo,lco->kc", innov_win[:, reach], gain, precision=lax.Precision.HIGHEST
        )
        return cell_blk + increment

    fresh = lax.map(
        update_block,
        (blocks.transpose(1, 0, 2), state_mean, loc_obs[batch_no, 0], loc_tile[batch_no, 0]),
    )
    return fresh.transpose(1, 0, 2).reshape(K, CB_DEV * BLK)


def per_device(
    states, obs_values, obs_weights, obs_cell, op_select, op_table, loc_obs, loc_tile, loc_tiles
):
    ensemble = states
    window_obs = window(observe_members(ensemble, obs_cell, op_select, op_table, 0))
    obs_anom, innov = prepare(window_obs, obs_values, obs_weights, 0)
    cells = to_cells(ensemble)
    cells = update_cells(cells, obs_anom, innov, loc_obs, loc_tile, loc_tiles, 0)
    window_obs = window(observe_owners(cells, obs_cell, op_select, op_table, 1))
    obs_anom, innov = prepare(window_obs, obs_values, obs_weights, 1)
    cells = update_cells(cells, obs_anom, innov, loc_obs, loc_tile, loc_tiles, 1)
    ensemble = to_members(cells)
    return ensemble


def solution(mesh):
    placed = (
        P("member", "space"),
        P(),
        P(),
        P(None, "space", None),
        P(None, "space", None),
        P(),
        P(None, "space", "member", None),
        P(None, "space", "member", None),
        P(),
    )
    return jax.shard_map(
        per_device, mesh=mesh, in_specs=placed, out_specs=P("member", "space"), check_vma=False
    )
```

profile of v0, /device:TPU:0, one launch (start us, length us, event | category | flops | bytes accessed | tf_op | source)
XLA Modules:
  0.0 793.8 jit_solution(15951240218992025015)
XLA Ops:
  18.9 7.3 all-to-all-start
  26.2 88.9 %all-gather.2.cloned.1.call-done = f32[1024,512]{0,1:T(8,128)} async-done(((f32[128,512]{0,1:T(8,128)}), f32[1024,512]{0,1:T(8,128)}) %all-gather.2.cloned.1.call-update) | async-done | bytes 2097168 | tf_op jit(solution)/shard_map/all_gather | solution.py:55
  134.5 27.0 %collective-permute-done = f32[1024,512]{0,1:T(8,128)} collective-permute-done((f32[1024,512]{0,1:T(8,128)}, f32[1024,512]{0,1:T(8,128)}, u32[]{:S(2)}, u32[]{:S(2)}) %collective-permute-start) | collective-permute-done | bytes 2097184 | tf_op jit(solution)/shard_map/ppermute | solution.py:19
  164.9 6.6 multiply_subtract_fusion.1
  171.5 6.5 copy.82
  178.1 6.6 copy.83
  186.5 169.5 %while.20 = (s32[]{:T(128)}, f32[6,1024,128]{2,1,0:T(8,128)}, f32[6,1024,128]{1,2,0:T(8,128)}, s32[6,8]{1,0:T(8,128)S(1)}, f32[1024,12,128]{2,0,1:T(8,128)}, /*i...) while((s32[]{:T(128)}, f32[6,1024,128]{2,1,0:T(8,128)}, ...), condition=%wide.region_3.4_spmd, body=%wide.region_2.3_spmd.sunk | while | flops 3221751808 | bytes 32516496 | solution.py:98
  194.3 8.5 %fusion.107 = f32[8,128,128]{1,2,0:T(8,128)S(1)} fusion(f32[8,128,128]{1,2,0:T(8,128)S(1)} %copy.108, f32[8,1024,128]{2,1,0:T(8,128)} %gather_fusion.1, f32[1,1024,128]{2,1,0:T(8,128)S(1)} %copy.109, f32[128]{0:T(128)S(1)} %fusion.106), kind=kOutput, calls=%fused_computation.20.clone.1 | convolution fusion | flops 1611005952 | bytes 5767680 | tf_op jit(solution)/shard_map/while/body/eval_jaxpr/kc,klo->lco/dot_general | solution.py:89
  222.5 8.5 %fusion.107 = f32[8,128,128]{1,2,0:T(8,128)S(1)} fusion(f32[8,128,128]{1,2,0:T(8,128)S(1)} %copy.108, f32[8,1024,128]{2,1,0:T(8,128)} %gather_fusion.1, f32[1,1024,128]{2,1,0:T(8,128)S(1)} %copy.109, f32[128]{0:T(128)S(1)} %fusion.106), kind=kOutput, calls=%fused_computation.20.clone.1 | convolution fusion | flops 1611005952 | bytes 5767680 | tf_op jit(solution)/shard_map/while/body/eval_jaxpr/kc,klo->lco/dot_general | solution.py:89
  250.8 8.5 %fusion.107 = f32[8,128,128]{1,2,0:T(8,128)S(1)} fusion(f32[8,128,128]{1,2,0:T(8,128)S(1)} %copy.108, f32[8,1024,128]{2,1,0:T(8,128)} %gather_fusion.1, f32[1,1024,128]{2,1,0:T(8,128)S(1)} %copy.109, f32[128]{0:T(128)S(1)} %fusion.106), kind=kOutput, calls=%fused_computation.20.clone.1 | convolution fusion | flops 1611005952 | bytes 5767680 | tf_op jit(solution)/shard_map/while/body/eval_jaxpr/kc,klo->lco/dot_general | solution.py:89
  279.0 8.5 %fusion.107 = f32[8,128,128]{1,2,0:T(8,128)S(1)} fusion(f32[8,128,128]{1,2,0:T(8,128)S(1)} %copy.108, f32[8,1024,128]{2,1,0:T(8,128)} %gather_fusion.1, f32[1,1024,128]{2,1,0:T(8,128)S(1)} %copy.109, f32[128]{0:T(128)S(1)} %fusion.106), kind=kOutput, calls=%fused_computation.20.clone.1 | convolution fusion | flops 1611005952 | bytes 5767680 | tf_op jit(solution)/shard_map/while/body/eval_jaxpr/kc,klo->lco/dot_general | solution.py:89
  307.3 8.5 %fusion.107 = f32[8,128,128]{1,2,0:T(8,128)S(1)} fusion(f32[8,128,128]{1,2,0:T(8,128)S(1)} %copy.108, f32[8,1024,128]{2,1,0:T(8,128)} %gather_fusion.1, f32[1,1024,128]{2,1,0:T(8,128)S(1)} %copy.109, f32[128]{0:T(128)S(1)} %fusion.106), kind=kOutput, calls=%fused_computation.20.clone.1 | convolution fusion | flops 1611005952 | bytes 5767680 | tf_op jit(solution)/shard_map/while/body/eval_jaxpr/kc,klo->lco/dot_general | solution.py:89
  335.5 8.5 %fusion.107 = f32[8,128,128]{1,2,0:T(8,128)S(1)} fusion(f32[8,128,128]{1,2,0:T(8,128)S(1)} %copy.108, f32[8,1024,128]{2,1,0:T(8,128)} %gather_fusion.1, f32[1,1024,128]{2,1,0:T(8,128)S(1)} %copy.109, f32[128]{0:T(128)S(1)} %fusion.106), kind=kOutput, calls=%fused_computation.20.clone.1 | convolution fusion | flops 1611005952 | bytes 5767680 | tf_op jit(solution)/shard_map/while/body/eval_jaxpr/kc,klo->lco/dot_general | solution.py:89
  364.8 102.8 %all-reduce.2.cloned.1.call-done = f32[1024,512]{0,1:T(8,128)} async-done(((f32[1024,512]{0,1:T(8,128)}), f32[1024,512]{0,1:T(8,128)}) %all-reduce.2.cloned.1.call-update) | async-done | bytes 2097168 | tf_op jit(solution)/shard_map/psum | solution.py:68
  472.8 41.3 %collective-permute-done.2 = f32[1024,512]{0,1:T(8,128)} collective-permute-done((f32[1024,512]{0,1:T(8,128)}, f32[1024,512]{0,1:T(8,128)}, u32[]{:S(2)}, u32[]{:S(2)}) %collective-permute-start.2) | collective-permute-done | bytes 2097184 | tf_op jit(solution)/shard_map/ppermute | solution.py:19
  517.4 6.6 multiply_subtract_fusion
  524.0 6.6 copy.86
  530.6 6.5 copy.87
  539.0 162.1 %while.21 = (s32[]{:T(128)}, f32[6,1024,128]{2,1,0:T(8,128)}, f32[6,1024,128]{2,1,0:T(8,128)}, s32[6,8]{1,0:T(8,128)S(1)}, f32[1024,12,128]{2,0,1:T(8,128)}, /*i...) while((s32[]{:T(128)}, f32[6,1024,128]{2,1,0:T(8,128)}, ...), condition=%wide.region_8.9_spmd, body=%wide.region_7.8_spmd.sunk | while | flops 3221751808 | bytes 30419852 | solution.py:98
  545.4 8.6 %fusion.115 = f32[8,128,128]{1,2,0:T(8,128)S(1)} fusion(f32[8,128,128]{1,2,0:T(8,128)S(1)} %copy.110, f32[8,1024,128]{2,1,0:T(8,128)} %gather_fusion.4, f32[6,1024,128]{2,1,0:T(8,128)} %get-tuple-element.404, s32[]{:T(128)} %get-tuple-element.392, f32[128]{0:T(128)S(1)} %fusion.114), kind=kOutput, calls=%fused_computation.47.clone.1 | convolution fusion | flops 1611005952 | bytes 5768192 | tf_op jit(solution)/shard_map/while/body/eval_jaxpr/kc,klo->lco/dot_general | solution.py:89
  559.5 6.5 fusion.116
  572.4 8.6 %fusion.115 = f32[8,128,128]{1,2,0:T(8,128)S(1)} fusion(f32[8,128,128]{1,2,0:T(8,128)S(1)} %copy.110, f32[8,1024,128]{2,1,0:T(8,128)} %gather_fusion.4, f32[6,1024,128]{2,1,0:T(8,128)} %get-tuple-element.404, s32[]{:T(128)} %get-tuple-element.392, f32[128]{0:T(128)S(1)} %fusion.114), kind=kOutput, calls=%fused_computation.47.clone.1 | convolution fusion | flops 1611005952 | bytes 5768192 | tf_op jit(solution)/shard_map/while/body/eval_jaxpr/kc,klo->lco/dot_general | solution.py:89
  586.5 6.5 fusion.116
  599.4 8.6 %fusion.115 = f32[8,128,128]{1,2,0:T(8,128)S(1)} fusion(f32[8,128,128]{1,2,0:T(8,128)S(1)} %copy.110, f32[8,1024,128]{2,1,0:T(8,128)} %gather_fusion.4, f32[6,1024,128]{2,1,0:T(8,128)} %get-tuple-element.404, s32[]{:T(128)} %get-tuple-element.392, f32[128]{0:T(128)S(1)} %fusion.114), kind=kOutput, calls=%fused_computation.47.clone.1 | convolution fusion | flops 1611005952 | bytes 5768192 | tf_op jit(solution)/shard_map/while/body/eval_jaxpr/kc,klo->lco/dot_general | solution.py:89
  613.5 6.5 fusion.116
  626.4 8.6 %fusion.115 = f32[8,128,128]{1,2,0:T(8,128)S(1)} fusion(f32[8,128,128]{1,2,0:T(8,128)S(1)} %copy.110, f32[8,1024,128]{2,1,0:T(8,128)} %gather_fusion.4, f32[6,1024,128]{2,1,0:T(8,128)} %get-tuple-element.404, s32[]{:T(128)} %get-tuple-element.392, f32[128]{0:T(128)S(1)} %fusion.114), kind=kOutput, calls=%fused_computation.47.clone.1 | convolution fusion | flops 1611005952 | bytes 5768192 | tf_op jit(solution)/shard_map/while/body/eval_jaxpr/kc,klo->lco/dot_general | solution.py:89
  640.5 6.5 fusion.116
  653.4 8.6 %fusion.115 = f32[8,128,128]{1,2,0:T(8,128)S(1)} fusion(f32[8,128,128]{1,2,0:T(8,128)S(1)} %copy.110, f32[8,1024,128]{2,1,0:T(8,128)} %gather_fusion.4, f32[6,1024,128]{2,1,0:T(8,128)} %get-tuple-element.404, s32[]{:T(128)} %get-tuple-element.392, f32[128]{0:T(128)S(1)} %fusion.114), kind=kOutput, calls=%fused_computation.47.clone.1 | convolution fusion | flops 1611005952 | bytes 5768192 | tf_op jit(solution)/shard_map/while/body/eval_jaxpr/kc,klo->lco/dot_general | solution.py:89
  667.5 6.5 fusion.116
  680.4 8.6 %fusion.115 = f32[8,128,128]{1,2,0:T(8,128)S(1)} fusion(f32[8,128,128]{1,2,0:T(8,128)S(1)} %copy.110, f32[8,1024,128]{2,1,0:T(8,128)} %gather_fusion.4, f32[6,1024,128]{2,1,0:T(8,128)} %get-tuple-element.404, s32[]{:T(128)} %get-tuple-element.392, f32[128]{0:T(128)S(1)} %fusion.114), kind=kOutput, calls=%fused_computation.47.clone.1 | convolution fusion | flops 1611005952 | bytes 5768192 | tf_op jit(solution)/shard_map/while/body/eval_jaxpr/kc,klo->lco/dot_general | solution.py:89
  694.6 6.5 fusion.116
  707.9 75.6 %all_to_all.35 = f32[8,128,768]{1,2,0:T(8,128)} all-to-all(f32[8,128,768]{1,2,0:T(8,128)S(1)} %copy.89), channel_id=1, replica_groups=mesh['member'=8,'space'=4] {'member'}, dimensions={0} | all-to-all | bytes 6291456 | tf_op jit(solution)/shard_map/all_to_all | solution.py:76
  (197 shorter events, 255.9 us)
Async XLA Ops:
  6.5 10.3 %copy-start = (f32[8,128,128]{2,1,0:T(8,128)S(1)}, f32[8,128,128]{2,1,0:T(8,128)}, u32[]{:S(2)}) copy-start(f32[8,128,128]{2,1,0:T(8,128)} %param.18) | copy-start | bytes 1572868
  6.5 108.6 %all-gather.2.cloned.1.call-start = ((), (), s32[]{:S(2)}) async-start(), calls=%async_computation.2 | async-start | bytes 2359296 | tf_op jit(solution)/shard_map/all_gather | solution.py:55
  10.8 3.5 copy-start.9
  14.4 102.5 %copy-start.5 = (f32[2,2048]{1,0:T(2,128)S(1)}, f32[2,2048]{1,0:T(2,128)}, u32[]{:S(2)}) copy-start(f32[2,2048]{1,0:T(2,128)} %param.14) | copy-start | bytes 49156
  14.4 102.5 %copy-start.6 = (f32[2,2048]{1,0:T(2,128)S(1)}, f32[2,2048]{1,0:T(2,128)}, u32[]{:S(2)}) copy-start(f32[2,2048]{1,0:T(2,128)} %param.15) | copy-start | bytes 49156
  17.5 101.3 %copy-start.10 = (s32[2,1,4]{2,1,0:T(1,128)S(1)}, s32[2,1,4]{2,1,0:T(1,128)}, u32[]{:S(2)}) copy-start(s32[2,1,4]{2,1,0:T(1,128)} %param.16) | copy-start | bytes 100
  17.5 101.3 %copy-start.7 = (s32[2,1,6,8]{3,1,2,0:T(1,128)S(1)}, s32[2,1,6,8]{3,1,2,0:T(1,128)}, u32[]{:S(2)}) copy-start(s32[2,1,6,8]{3,1,2,0:T(1,128)} %param.20) | copy-start | bytes 1156
  17.5 101.3 %copy-start.8 = (s32[2,1,6,8]{3,1,2,0:T(1,128)S(1)}, s32[2,1,6,8]{3,1,2,0:T(1,128)}, u32[]{:S(2)}) copy-start(s32[2,1,6,8]{3,1,2,0:T(1,128)} %param.19) | copy-start | bytes 1156
  18.9 103.4 %all-to-all-start = ((f32[128,8,768]{0,2,1:T(8,128)}), f32[128,8,768]{0,2,1:T(8,128)}, u32[]{:S(2)}, u32[]{:S(2)}) async-start(f32[128,8,768]{0,2,1:T(8,128)} %bitcast.261), calls=%async_computation | async-start | bytes 6291456 | tf_op jit(solution)/shard_map/all_to_all | solution.py:72
  26.2 441.4 %all-reduce.2.cloned.1.call-start = ((), (), s32[]{:S(2)}) async-start(), calls=%async_computation.3 | async-start | bytes 4194304 | tf_op jit(solution)/shard_map/psum | solution.py:68
  115.1 46.4 %collective-permute-start = (f32[1024,512]{0,1:T(8,128)}, f32[1024,512]{0,1:T(8,128)}, u32[]{:S(2)}, u32[]{:S(2)}) collective-permute-start(f32[1024,512]{0,1:T(8,128)} %all-gather.2.cloned.1.call-done), channel_id=1, source_target_pairs={{0,1},{1,2},{2,3},{3,0},{4,5},{5,6},{6,7},{7,4},{8,9},{9,10},{10,1... | collective-permute-start | bytes 6291464 | tf_op jit(solution)/shard_map/ppermute | solution.py:19
  115.1 47.3 %collective-permute-start.1 = (f32[1024,512]{0,1:T(8,128)}, f32[1024,512]{0,1:T(8,128)}, u32[]{:S(2)}, u32[]{:S(2)}) collective-permute-start(f32[1024,512]{0,1:T(8,128)} %all-gather.2.cloned.1.call-done), channel_id=1, source_target_pairs={{1,0},{2,1},{3,2},{0,3},{5,4},{6,5},{7,6},{4,7},{9,8},{10,9},{11,1... | collective-permute-start | bytes 6291464 | tf_op jit(solution)/shard_map/ppermute | solution.py:21
  127.7 34.7 %copy-start.3 = (f32[1024,512]{0,1:T(8,128)S(1)}, f32[1024,512]{0,1:T(8,128)}, u32[]{:S(2)}) copy-start(f32[1024,512]{0,1:T(8,128)} %all-gather.2.cloned.1.call-done) | copy-start | bytes 6291460
  178.1 8.4 %copy-start.2 = (f32[8,128,128]{2,1,0:T(8,128)S(1)}, f32[8,128,128]{2,1,0:T(8,128)}, u32[]{:S(2)}) copy-start(f32[8,128,128]{2,1,0:T(8,128)} %param.21) | copy-start | bytes 1572868
  467.6 46.5 %collective-permute-start.2 = (f32[1024,512]{0,1:T(8,128)}, f32[1024,512]{0,1:T(8,128)}, u32[]{:S(2)}, u32[]{:S(2)}) collective-permute-start(f32[1024,512]{0,1:T(8,128)} %all-reduce.2.cloned.1.call-done), channel_id=1, source_target_pairs={{0,1},{1,2},{2,3},{3,0},{4,5},{5,6},{6,7},{7,4},{8,9},{9,10},{10,1... | collective-permute-start | bytes 6291464 | tf_op jit(solution)/shard_map/ppermute | solution.py:19
  467.6 47.2 %collective-permute-start.3 = (f32[1024,512]{0,1:T(8,128)}, f32[1024,512]{0,1:T(8,128)}, u32[]{:S(2)}, u32[]{:S(2)}) collective-permute-start(f32[1024,512]{0,1:T(8,128)} %all-reduce.2.cloned.1.call-done), channel_id=1, source_target_pairs={{1,0},{2,1},{3,2},{0,3},{5,4},{6,5},{7,6},{4,7},{9,8},{10,9},{11,1... | collective-permute-start | bytes 6291464 | tf_op jit(solution)/shard_map/ppermute | solution.py:21
  470.5 44.3 %copy-start.4 = (f32[1024,512]{0,1:T(8,128)S(1)}, f32[1024,512]{0,1:T(8,128)}, u32[]{:S(2)}) copy-start(f32[1024,512]{0,1:T(8,128)} %all-reduce.2.cloned.1.call-done) | copy-start | bytes 6291460
  707.8 79.1 %copy-start.1 = (f32[8,128,128]{2,1,0:T(8,128)S(1)}, f32[8,128,128]{2,1,0:T(8,128)}, u32[]{:S(2)}) copy-start(f32[8,128,128]{2,1,0:T(8,128)} %param.18) | copy-start | bytes 1572868
Sparse Core Ops, SparseCore 0:
  19.0 96.0 all-gather.1
  364.9 102.6 all-reduce.1
where the time goes:
time: 796 us; the launch traced here: 794 us
  waiting for transfers between devices  265 us (33%)
  local copies, waits for them, and re-layouts  219 us (28%)
  matrix products  186 us (23%)
  blocking collectives  75.6 us (9%)
  other arithmetic  23.5 us (3%)
  between operations  13.7 us (2%)
  starting transfers between devices  10.8 us (1%)
    psum x1, waiting for transfers between devices, observe_owners(): return lax.psum(observed.reshape(K, OB * BLK), 'member')  103 us
    dot_general x12, matrix products, update_block(): jnp.einsum('kc,klo->lco', state_anom, chosen, precision=lax.Precision.HIG...  102 us
    all_gather x1, waiting for transfers between devices, observe_members(): return lax.all_gather(observed, 'member', axis=0, tiled=True)  88.9 us
    dot_general x12, matrix products, update_block(): jnp.einsum('klo,lco->kc', innov_win[:, reach], gain, precision=lax.Precis...  77.6 us
    all_to_all x1, blocking collectives, to_members(): lax.all_to_all(cells, 'member', split_axis=0, concat_axis=1, tiled=True)  75.6 us
    ppermute x2, waiting for transfers between devices, with_halo(): lax.ppermute(tail, axis, [(i, (i + 1) % count) for i in range(count)])  68.4 us
    gather x12, local copies, waits for them, and re-layouts, update_block(): innov_win[:, reach]  67 us
    gather x12, local copies, waits for them, and re-layouts, update_block(): chosen = anom_win[:, reach]  67 us
  transfers between devices with their start and end apart: 7, of which 7 were waited for; matrix products, arithmetic and copies ran while one was open for 2% of the time, Pallas kernels for 0%

commit v1 on v0

v1 whole, which is shorter than its diff:
```python
import functools

import jax
import jax.numpy as jnp
from jax import lax
from jax.experimental import pallas as pl
from jax.experimental.pallas import tpu as pltpu
from jax.sharding import PartitionSpec as P

BLK = 128
NT_DIMS = (((1,), (1,)), ((), ()))


def split(x):
    hi = x.astype(jnp.bfloat16)
    lo = (x - hi.astype(jnp.float32)).astype(jnp.bfloat16)
    return hi, lo


def dot(a, b):
    return jnp.dot(a, b, preferred_element_type=jnp.float32)


def dot_nt(a, b):
    return lax.dot_general(a, b, NT_DIMS, preferred_element_type=jnp.float32)


def update_kernel(nb, ob, loc, picks, *refs):
    reach_ref, tile_ref, op_ref = refs[:3]
    refs = refs[3:]
    cells_ref, refs = refs[0], refs[1:]
    if picks:
        picked_ref, table_ref, refs = refs[0], refs[1], refs[2:]
    prev_ref, own_ref, next_ref, values_ref, weights_ref, tiles_ref = refs[:6]
    refs = refs[6:]
    out_ref, refs = refs[0], refs[1:]
    if picks:
        obs_ref, refs = refs[0], refs[1:]
    hi_ref, lo_ref, d_ref, acc_ref = refs
    members = cells_ref.shape[0]
    n = pl.program_id(0)

    @pl.when(n == 0)
    def _():
        for slab, ref in enumerate((prev_ref, own_ref, next_ref)):
            for o in range(ob):
                j = slab * ob + o
                block = ref[:, o * BLK:(o + 1) * BLK]
                mean = jnp.sum(block, axis=0, keepdims=True) * (1.0 / members)
                hi, lo = split(block - mean)
                hi_ref[j] = hi
                lo_ref[j] = lo
                d_ref[j] = weights_ref[j] * (values_ref[j] - mean)

    def update(cell):
        mean = jnp.sum(cell, axis=0, keepdims=True) * (1.0 / members)
        hi, lo = split(jnp.transpose(cell - mean))
        both = jnp.concatenate([hi, lo], axis=0)
        ones = []
        for pair in range(loc // 2):
            first, second = reach_ref[n, 2 * pair], reach_ref[n, 2 * pair + 1]
            obs_hi = jnp.concatenate([hi_ref[first], hi_ref[second]], axis=1)
            obs_lo = jnp.concatenate([lo_ref[first], lo_ref[second]], axis=1)
            part = dot(both, obs_hi)
            cov = part[:BLK] + part[BLK:] + dot(hi, obs_lo)
            tile = jnp.concatenate(
                [tiles_ref[tile_ref[n, 2 * pair]], tiles_ref[tile_ref[n, 2 * pair + 1]]], axis=1
            )
            gain = tile * (cov * (1.0 / (members - 1)))
            d = jnp.concatenate([d_ref[first], d_ref[second]], axis=1)
            w = jnp.concatenate([weights_ref[first], weights_ref[second]], axis=1)
            ones.append(jnp.sum(gain * d, axis=1, keepdims=True))
            gain_hi, gain_lo = split(gain * (-0.5 * w))
            step = dot_nt(obs_hi, jnp.concatenate([gain_hi, gain_lo], axis=0))
            step = step[:, :BLK] + step[:, BLK:] + dot_nt(obs_lo, gain_hi)
            if pair == 0:
                acc_ref[...] = step
            else:
                acc_ref[...] += step
        shift = functools.reduce(jnp.add, ones)
        row = jnp.transpose(jnp.broadcast_to(shift, (BLK, BLK)))[:1]
        return cell + (acc_ref[...] + row)

    if picks:
        @pl.when(n < nb)
        def _():
            out_ref[...] = update(cells_ref[...])

        @pl.when(n >= nb)
        def _():
            fresh_hi, fresh_lo = split(update(picked_ref[...]))
            op_hi, op_lo = split(table_ref[op_ref[jnp.maximum(n - nb, 0)]])
            part = dot_nt(fresh_hi, jnp.concatenate([op_hi, op_lo], axis=0))
            obs_ref[...] = part[:, :BLK] + part[:, BLK:] + dot_nt(fresh_lo, op_hi)
    else:
        out_ref[...] = update(cells_ref[...])


def update_cells(cells, window, values, weights, tiles, reach, tile_pick, picked=None, table=None, ops=None):
    members = cells.shape[0]
    nb = cells.shape[1] // BLK
    ob = window[0].shape[1] // BLK
    loc = reach.shape[1]
    picks = 0 if picked is None else ob
    whole = pl.BlockSpec(memory_space=pltpu.VMEM)
    block = pl.BlockSpec((members, BLK), lambda n, *_: (0, jnp.minimum(n, nb - 1)))
    late = pl.BlockSpec((members, BLK), lambda n, *_: (0, jnp.maximum(n - nb, 0)))
    if ops is None:
        ops = jnp.zeros((ob,), jnp.int32)
    args = [reach, tile_pick, ops, cells]
    in_specs = [block]
    out_shape = [jax.ShapeDtypeStruct(cells.shape, jnp.float32)]
    out_specs = [block]
    if picks:
        args += [picked, table]
        in_specs += [late, whole]
        out_shape.append(jax.ShapeDtypeStruct((members, ob * BLK), jnp.float32))
        out_specs.append(late)
    args += [*window, values, weights, tiles]
    in_specs += [whole] * 6
    return pl.pallas_call(
        functools.partial(update_kernel, nb, ob, loc, picks),
        grid_spec=pltpu.PrefetchScalarGridSpec(
            num_scalar_prefetch=3,
            grid=(nb + picks,),
            in_specs=in_specs,
            out_specs=out_specs,
            scratch_shapes=[
                pltpu.VMEM((3 * ob, members, BLK), jnp.bfloat16),
                pltpu.VMEM((3 * ob, members, BLK), jnp.bfloat16),
                pltpu.VMEM((3 * ob, 1, BLK), jnp.float32),
                pltpu.VMEM((members, BLK), jnp.float32),
            ],
        ),
        out_shape=out_shape,
        compiler_params=pltpu.CompilerParams(
            dimension_semantics=("arbitrary",), vmem_limit_bytes=56 * 1024 * 1024
        ),
    )(*args)


def window_values(flat_row, width):
    space_n = lax.axis_size("space")
    by_slab = flat_row.reshape(space_n, width)
    pick = (lax.axis_index("space") - 1 + jnp.arange(3, dtype=jnp.int32)) % space_n
    return by_slab[pick].reshape(3 * width // BLK, 1, BLK)


def halo(own):
    count = lax.axis_size("space")
    up = [(i, (i + 1) % count) for i in range(count)]
    down = [((i + 1) % count, i) for i in range(count)]
    return lax.ppermute(own, "space", up), own, lax.ppermute(own, "space", down)


def per_device(
    states, obs_values, obs_weights, obs_cell, op_select, op_table, loc_obs, loc_tile, loc_tiles
):
    share, width = states.shape
    ob = obs_cell.shape[2]
    obs_w = ob * BLK
    member_n = lax.axis_size("member")
    nb, loc = loc_obs.shape[2:]

    def pick(batch_no):
        return [
            lax.dynamic_slice_in_dim(states, obs_cell[batch_no, 0, o] * BLK, BLK, axis=1)
            for o in range(ob)
        ]

    first = jnp.stack(pick(0))
    observed = jnp.einsum(
        "okc,opc->kop", first, op_table[op_select[0, 0]], precision=lax.Precision.HIGHEST
    ).reshape(share, obs_w)
    second = jnp.concatenate(pick(1), axis=1)
    ints = jnp.stack([loc_obs[0, 0], loc_tile[0, 0]]).astype(jnp.float32).reshape(-1)
    extra = -(-ints.shape[0] // (2 * obs_w * 8)) * 8
    ints = jnp.pad(ints, (0, extra * 2 * obs_w - ints.shape[0])).reshape(extra, 2 * obs_w)
    sent = jnp.concatenate([jnp.concatenate([observed, second], axis=1), ints], axis=0)
    got = lax.all_gather(sent, "member", axis=0)
    own = got[:, :share, :obs_w].reshape(member_n * share, obs_w)
    picked = got[:, :share, obs_w:].reshape(member_n * share, obs_w)
    table = got[:, share:].reshape(member_n, -1)[:, : 2 * nb * loc]
    table = table.reshape(member_n, 2, nb, loc).astype(jnp.int32)
    table = table.transpose(1, 0, 2, 3).reshape(2, member_n * nb, loc)
    late = table[:, obs_cell[1, 0]]
    reach = jnp.concatenate([loc_obs[0, 0], late[0]], axis=0)
    tile_pick = jnp.concatenate([loc_tile[0, 0], late[1]], axis=0)

    cells = lax.all_to_all(states, "member", split_axis=1, concat_axis=0, tiled=True)
    cells, observed = update_cells(
        cells, halo(own), window_values(obs_values[0], obs_w), window_values(obs_weights[0], obs_w),
        loc_tiles, reach, tile_pick, picked, op_table, op_select[1, 0],
    )
    (cells,) = update_cells(
        cells, halo(observed), window_values(obs_values[1], obs_w),
        window_values(obs_weights[1], obs_w), loc_tiles, loc_obs[1, 0], loc_tile[1, 0],
    )
    return lax.all_to_all(cells, "member", split_axis=0, concat_axis=1, tiled=True)


def solution(mesh):
    placed = (
        P("member", "space"),
        P(),
        P(),
        P(None, "space", None),
        P(None, "space", None),
        P(),
        P(None, "space", "member", None),
        P(None, "space", "member", None),
        P(),
    )
    return jax.shard_map(
        per_device, mesh=mesh, in_specs=placed, out_specs=P("member", "space"), check_vma=False
    )
```

time: 796 us -> 411 us (0.52)
  local copies, waits for them, and re-layouts: 219 us -> 27.2 us
  matrix products: 186 us -> 1.37 us
  Pallas kernels: 0 us -> 64.4 us
  waiting for transfers between devices: 265 us -> 211 us
  other arithmetic: 23.5 us -> 3.84 us
    dot_general x26 -> x1, matrix products: 186 us -> 1.37 us  [per_device(): jnp.einsum('okc,opc->kop', first, op_table[op_select[0, 0]], precision=la...]
    gather x56 -> x6, local copies, waits for them, and re-layouts: 153 us -> 4.42 us  [the longest x4 2.24 us: window_values(): return by_slab[pick].reshape(3 * width // BLK, 1, BLK)]
    psum x1 -> x0, waiting for transfers between devices: 103 us -> none  [observe_owners(): return lax.psum(observed.reshape(K, OB * BLK), 'member')]
    pallas_call x0 -> x2, Pallas kernels: none -> 64.4 us  [update_cells(): pl.pallas_call(functools.partial(update_kernel, nb, ob, loc, picks), grid...]
    all_gather x1, waiting for transfers between devices: 88.9 us -> 127 us  [per_device(): got = lax.all_gather(sent, 'member', axis=0)]
    while x4 -> x0, local copies, waits for them, and re-layouts: 26.3 us -> none  [update_cells(): lax.map(update_block, (blocks.transpose(1, 0, 2), state_mean, loc_obs[bat...]
    ppermute x4, waiting for transfers between devices: 70 us -> 84.7 us  [the longest x2 82.9 us: halo(): lax.ppermute(own, 'space', down)]
    sub x2 -> x0, other arithmetic: 13.2 us -> none  [prepare(): innov = weights * (values - obs_mean) - 0.5 * weights * obs_anom]
  transfers between devices with their start and end apart: 7 -> 6, of which waited for: 7 -> 5; matrix products, arithmetic and copies ran while one was open for 2% -> 4% of each run, Pallas kernels for 0% -> 0%
where the time goes in v1:
time: 411 us; the launch traced here: 410 us
  waiting for transfers between devices  211 us (51%)
  blocking collectives  74.4 us (18%)
  Pallas kernels  64.4 us (16%)
  local copies, waits for them, and re-layouts  27.2 us (7%)
  between operations  18.6 us (5%)
  starting transfers between devices  9.42 us (2%)
    all_gather x1, waiting for transfers between devices, per_device(): got = lax.all_gather(sent, 'member', axis=0)  127 us
    ppermute x2, waiting for transfers between devices, halo(): lax.ppermute(own, 'space', down)  82.9 us
    all_to_all x1, blocking collectives, per_device(): lax.all_to_all(cells, 'member', split_axis=0, concat_axis=1, tiled=True)  74.4 us
    pallas_call x2, Pallas kernels, update_cells(): pl.pallas_call(functools.partial(update_kernel, nb, ob, loc, picks), grid...  64.4 us
  transfers between devices with their start and end apart: 6, of which 5 were waited for; matrix products, arithmetic and copies ran while one was open for 4% of the time, Pallas kernels for 0%

profile of v1, /device:TPU:0, one launch (start us, length us, event | category | flops | bytes accessed | tf_op | source)
XLA Modules:
  0.0 410.4 jit_solution(13028288918300895616)
XLA Ops:
  6.5 1.6 fusion.17
  13.1 0.7 fusion.9
  13.8 0.7 fusion.14
  14.7 1.6 gather_fusion
  16.3 1.0 dynamic-slice_bitcast_fusion.3
  17.3 1.4 fusion
  18.7 1.1 copy.40
  19.8 0.7 constant_dynamic-update-slice_fusion
  20.5 0.6 dynamic-slice_dynamic-update-slice_fusion.3
  21.1 0.6 dynamic-slice_dynamic-update-slice_fusion.2
  21.8 0.6 dynamic-slice_dynamic-update-slice_fusion.1
  22.4 0.6 dynamic-slice_dynamic-update-slice_fusion
  23.0 1.9 pad_maximum_fusion
  25.0 2.0 copy.61
  26.9 7.3 %all-to-all-start = ((f32[128,8,768]{2,0,1:T(8,128)}), f32[128,8,768]{2,0,1:T(8,128)S(1)}, u32[]{:S(2)}, u32[]{:S(2)}) async-start(f32[128,8,768]{2,0,1:T(8,128)} %bitcast.65), calls=%async_computation | async-start | bytes 6291456 | tf_op jit(solution)/shard_map/all_to_all | solution.py:190
  34.2 126.5 %all-gather.3.cloned.1.call-done = f32[1088,1024]{1,0:T(8,128)} async-done(((f32[136,1024]{1,0:T(8,128)}), f32[1088,1024]{1,0:T(8,128)}) %all-gather.3.cloned.1.call-update) | async-done | bytes 4456464 | tf_op jit(solution)/shard_map/all_gather | solution.py:180
  160.7 4.9 %fusion.13 = (f32[8,128,512]{2,1,0:T(8,128)}, f32[8,128,512]{2,1,0:T(8,128)}) fusion(f32[8,136,1024]{2,1,0:T(8,128)} %bitcast.74), kind=kLoop, calls=%fused_computation.55 | loop fusion | bytes 8388608 | tf_op jit(solution)/shard_map/slice | solution.py:181
  165.7 1.0 collective-permute-start.1
  167.4 0.6 reshape.169.refs_10_
  168.6 0.6 reshape.168.refs_9_
  169.7 1.0 slice_bitcast_fusion
  172.8 40.2 %collective-permute-done.1.refs_8_ = f32[1024,512]{1,0:T(8,128)} collective-permute-done((f32[1024,512]{1,0:T(8,128)}, f32[1024,512]{1,0:T(8,128)}, u32[]{:S(2)}, u32[]{:S(2)}) %collective-permute-start.1) | collective-permute-done | bytes 2097184 | tf_op jit(solution)/shard_map/ppermute | solution.py:153
  213.0 1.0 collective-permute-done.refs_6_
  214.0 36.5 %shard_map.91 = (f32[1024,768]{1,0:T(8,128)}, f32[1024,512]{1,0:T(8,128)}) custom-call(s32[10,8]{1,0:T(8,128)} %pad_add_fusion.refs_0_, s32[10,8]{1,0:T(8,128)} %pad_add_fusion.1.refs_1_, s32[4]{0:T(128)} %slice_bitcast_fusion.1.refs_2_, f32[1024,768]{1,0:T(8,128)} %bitcast.72, f32[1024,512]{1,0:T(8,128)} %bitcast.73, f32[8,128,128]{2,1,0:T(8,128)} %refs_5_.1, ...), custom_call_target="tpu_custom_call" | custom-call | tf_op jit(solution)/shard_map/pallas_call | solution.py:121
  250.5 1.1 collective-permute-start.3
  253.3 0.6 reshape.171.refs_8_
  254.5 0.6 reshape.170.refs_7_
  255.1 42.7 %collective-permute-done.3.refs_6_ = f32[1024,512]{1,0:T(8,128)S(1)} collective-permute-done((f32[1024,512]{1,0:T(8,128)}, f32[1024,512]{1,0:T(8,128)S(1)}, u32[]{:S(2)}, u32[]{:S(2)}) %collective-permute-start.3) | collective-permute-done | bytes 2097184 | tf_op jit(solution)/shard_map/ppermute | solution.py:153
  297.9 0.8 collective-permute-done.2.refs_4_
  299.3 27.9 %shard_map.92 = f32[1024,768]{1,0:T(8,128)} custom-call(s32[6,8]{1,0:T(8,128)} %bitcast.82, s32[6,8]{1,0:T(8,128)} %bitcast.81, s32[4]{0:T(128)} %broadcast_11_refs_2_.2.refs_2_, f32[1024,768]{1,0:T(8,128)} %get-tuple-element.7.refs_3_, f32[1024,512]{1,0:T(8,128)} %collective-permute-done.2.refs_4_, f32[1024,512]{1,0:T(8,128)} %get-tuple-element.8.refs_5_, ...), custom_call_target="tpu_custom_call" | custom-call | tf_op jit(solution)/shard_map/pallas_call | solution.py:121
  327.2 74.4 %all_to_all.38 = f32[8,128,768]{2,1,0:T(8,128)S(1)} all-to-all(f32[8,128,768]{2,1,0:T(8,128)} %bitcast.71), channel_id=1, replica_groups=mesh['member'=8,'space'=4] {'member'}, dimensions={0} | all-to-all | bytes 6291456 | tf_op jit(solution)/shard_map/all_to_all | solution.py:199
  401.6 2.0 copy.54
  (49 shorter events, 6.9 us)
Async XLA Ops:
  6.5 14.0 %copy-start.1 = (f32[128,6144]{1,0:T(8,128)S(1)}, f32[128,6144]{1,0:T(8,128)}, u32[]{:S(2)}) copy-start(f32[128,6144]{1,0:T(8,128)} %param.9) | copy-start | bytes 9437188
  6.5 154.2 %all-gather.3.cloned.1.call-start = ((), (), s32[]{:S(2)}) async-start(), calls=%async_computation.2 | async-start | bytes 5013504 | tf_op jit(solution)/shard_map/all_gather | solution.py:180
  26.9 145.8 %all-to-all-start = ((f32[128,8,768]{2,0,1:T(8,128)}), f32[128,8,768]{2,0,1:T(8,128)S(1)}, u32[]{:S(2)}, u32[]{:S(2)}) async-start(f32[128,8,768]{2,0,1:T(8,128)} %bitcast.65), calls=%async_computation | async-start | bytes 6291456 | tf_op jit(solution)/shard_map/all_to_all | solution.py:190
  160.7 6.0 %copy-start.3 = (f32[2,2048]{1,0:T(2,128)S(1)}, f32[2,2048]{1,0:T(2,128)}, u32[]{:S(2)}) copy-start(f32[2,2048]{1,0:T(2,128)} %param.11) | copy-start | bytes 49156
  160.7 6.0 %copy-start.4 = (f32[2,2048]{1,0:T(2,128)S(1)}, f32[2,2048]{1,0:T(2,128)}, u32[]{:S(2)}) copy-start(f32[2,2048]{1,0:T(2,128)} %param.10) | copy-start | bytes 49156
  160.7 8.5 %copy-start.5 = (s32[2,1,4]{2,1,0:T(1,128)S(1)}, s32[2,1,4]{2,1,0:T(1,128)}, u32[]{:S(2)}) copy-start(s32[2,1,4]{2,1,0:T(1,128)} %param.13) | copy-start | bytes 100
  165.7 47.3 %collective-permute-start.1 = (f32[1024,512]{1,0:T(8,128)}, f32[1024,512]{1,0:T(8,128)}, u32[]{:S(2)}, u32[]{:S(2)}) collective-permute-start(f32[1024,512]{1,0:T(8,128)} %bitcast.32.refs_7_), channel_id=1, source_target_pairs={{1,0},{2,1},{3,2},{0,3},{5,4},{6,5},{7,6},{4,7},{9,8},{10,9},{11,1... | collective-permute-start | bytes 6291464 | tf_op jit(solution)/shard_map/ppermute | solution.py:153
  166.7 47.3 %collective-permute-start = (f32[1024,512]{1,0:T(8,128)}, f32[1024,512]{1,0:T(8,128)}, u32[]{:S(2)}, u32[]{:S(2)}) collective-permute-start(f32[1024,512]{1,0:T(8,128)} %bitcast.32.refs_7_), channel_id=1, source_target_pairs={{0,1},{1,2},{2,3},{3,0},{4,5},{5,6},{6,7},{7,4},{8,9},{9,10},{10,1... | collective-permute-start | bytes 6291464 | tf_op jit(solution)/shard_map/ppermute | solution.py:153
  172.8 41.2 %copy-start = (f32[128,8,768]{2,0,1:T(8,128)}, f32[128,8,768]{2,0,1:T(8,128)S(1)}, u32[]{:S(2)}) copy-start(f32[128,8,768]{2,0,1:T(8,128)S(1)} %all-to-all-done) | copy-start | bytes 9437188
  250.5 47.4 %collective-permute-start.3 = (f32[1024,512]{1,0:T(8,128)}, f32[1024,512]{1,0:T(8,128)S(1)}, u32[]{:S(2)}, u32[]{:S(2)}) collective-permute-start(f32[1024,512]{1,0:T(8,128)} %get-tuple-element.8.refs_5_), channel_id=1, source_target_pairs={{1,0},{2,1},{3,2},{0,3},{5,4},{6,5},{7,6},{4,7},{9,8},{10,9},{11,1... | collective-permute-start | bytes 6291464 | tf_op jit(solution)/shard_map/ppermute | solution.py:153
  251.6 47.1 %collective-permute-start.2 = (f32[1024,512]{1,0:T(8,128)}, f32[1024,512]{1,0:T(8,128)}, u32[]{:S(2)}, u32[]{:S(2)}) collective-permute-start(f32[1024,512]{1,0:T(8,128)} %get-tuple-element.8.refs_5_), channel_id=1, source_target_pairs={{0,1},{1,2},{2,3},{3,0},{4,5},{5,6},{6,7},{7,4},{8,9},{9,10},{10,1... | collective-permute-start | bytes 6291464 | tf_op jit(solution)/shard_map/ppermute | solution.py:153
  297.9 1.4 copy-start.2
Sparse Core Ops, SparseCore 0:
  25.1 135.5 all-gather.2

commit v2 on v1

--- a/solution.py
+++ b/solution.py
@@ -25,17 +25,15 @@
     return lax.dot_general(a, b, NT_DIMS, preferred_element_type=jnp.float32)
 
 
-def update_kernel(nb, ob, loc, picks, *refs):
+def update_kernel(ob, loc, picks, *refs):
     reach_ref, tile_ref, op_ref = refs[:3]
     refs = refs[3:]
     cells_ref, refs = refs[0], refs[1:]
     if picks:
-        picked_ref, table_ref, refs = refs[0], refs[1], refs[2:]
+        table_ref, refs = refs[0], refs[1:]
     prev_ref, own_ref, next_ref, values_ref, weights_ref, tiles_ref = refs[:6]
     refs = refs[6:]
     out_ref, refs = refs[0], refs[1:]
-    if picks:
-        obs_ref, refs = refs[0], refs[1:]
     hi_ref, lo_ref, d_ref, acc_ref = refs
     members = cells_ref.shape[0]
     n = pl.program_id(0)
@@ -82,49 +80,33 @@
         return cell + (acc_ref[...] + row)
 
     if picks:
-        @pl.when(n < nb)
-        def _():
-            out_ref[...] = update(cells_ref[...])
-
-        @pl.when(n >= nb)
-        def _():
-            fresh_hi, fresh_lo = split(update(picked_ref[...]))
-            op_hi, op_lo = split(table_ref[op_ref[jnp.maximum(n - nb, 0)]])
-            part = dot_nt(fresh_hi, jnp.concatenate([op_hi, op_lo], axis=0))
-            obs_ref[...] = part[:, :BLK] + part[:, BLK:] + dot_nt(fresh_lo, op_hi)
+        fresh_hi, fresh_lo = split(update(cells_ref[...]))
+        op_hi, op_lo = split(table_ref[op_ref[n]])
+        part = dot_nt(fresh_hi, jnp.concatenate([op_hi, op_lo], axis=0))
+        out_ref[...] = part[:, :BLK] + part[:, BLK:] + dot_nt(fresh_lo, op_hi)
     else:
         out_ref[...] = update(cells_ref[...])
 
 
-def update_cells(cells, window, values, weights, tiles, reach, tile_pick, picked=None, table=None, ops=None):
+def update_cells(cells, window, values, weights, tiles, reach, tile_pick, table=None, ops=None):
     members = cells.shape[0]
     nb = cells.shape[1] // BLK
     ob = window[0].shape[1] // BLK
     loc = reach.shape[1]
-    picks = 0 if picked is None else ob
+    picks = table is not None
     whole = pl.BlockSpec(memory_space=pltpu.VMEM)
-    block = pl.BlockSpec((members, BLK), lambda n, *_: (0, jnp.minimum(n, nb - 1)))
-    late = pl.BlockSpec((members, BLK), lambda n, *_: (0, jnp.maximum(n - nb, 0)))
+    block = pl.BlockSpec((members, BLK), lambda n, *_: (0, n))
     if ops is None:
         ops = jnp.zeros((ob,), jnp.int32)
-    args = [reach, tile_pick, ops, cells]
-    in_specs = [block]
-    out_shape = [jax.ShapeDtypeStruct(cells.shape, jnp.float32)]
-    out_specs = [block]
-    if picks:
-        args += [picked, table]
-        in_specs += [late, whole]
-        out_shape.append(jax.ShapeDtypeStruct((members, ob * BLK), jnp.float32))
-        out_specs.append(late)
+    args = [reach, tile_pick, ops, cells] + ([table] if picks else [])
     args += [*window, values, weights, tiles]
-    in_specs += [whole] * 6
     return pl.pallas_call(
-        functools.partial(update_kernel, nb, ob, loc, picks),
+        functools.partial(update_kernel, ob, loc, picks),
         grid_spec=pltpu.PrefetchScalarGridSpec(
             num_scalar_prefetch=3,
-            grid=(nb + picks,),
-            in_specs=in_specs,
-            out_specs=out_specs,
+            grid=(nb,),
+            in_specs=[block] + [whole] * (len(args) - 4),
+            out_specs=block,
             scratch_shapes=[
                 pltpu.VMEM((3 * ob, members, BLK), jnp.bfloat16),
                 pltpu.VMEM((3 * ob, members, BLK), jnp.bfloat16),
@@ -132,11 +114,192 @@
                 pltpu.VMEM((members, BLK), jnp.float32),
             ],
         ),
-        out_shape=out_shape,
+        out_shape=jax.ShapeDtypeStruct(cells.shape, jnp.float32),
         compiler_params=pltpu.CompilerParams(
             dimension_semantics=("arbitrary",), vmem_limit_bytes=56 * 1024 * 1024
         ),
+        cost_estimate=pl.CostEstimate(
+            flops=16 * nb * members * BLK * BLK * loc, bytes_accessed=32 << 20, transcendentals=0
+        ),
     )(*args)
+
+
+def gather_kernel(member_n, space_n, *refs):
+    ins, refs = refs[:3], refs[3:]
+    outs, refs = refs[:3], refs[3:]
+    prev_ref, next_ref, send_sem, recv_sem, halo_send, halo_recv, local_sem = refs
+    me = lax.axis_index("member")
+    slab = lax.axis_index("space")
+    line = member_n // 2
+    at, lane = me // 2, lax.rem(me, 2)
+    mate = at * 2 + 1 - lane
+    after = lax.rem(slab + 1, space_n)
+    before = lax.rem(slab + space_n - 1, space_n)
+
+    barrier = pltpu.get_barrier_semaphore()
+
+    def greet(member, space):
+        pl.semaphore_signal(
+            barrier, inc=1, device_id=(member, space), device_id_type=pl.DeviceIdType.MESH
+        )
+
+    greet(mate, slab)
+    greet(me, after)
+    greet(me, before)
+
+    @pl.when(at > 0)
+    def _():
+        greet(me - 2, slab)
+
+    @pl.when(at < line - 1)
+    def _():
+        greet(me + 2, slab)
+
+    pl.semaphore_wait(
+        barrier, 3 + jnp.where(at > 0, 1, 0) + jnp.where(at < line - 1, 1, 0)
+    )
+
+    def rows(ref, item, block):
+        size = ins[item].shape[0]
+        return ref.at[pl.ds(pl.multiple_of(block * size, 8), size)]
+
+    def hop(item, block, way, target, mine=False):
+        return pltpu.make_async_remote_copy(
+            src_ref=ins[item] if mine else rows(outs[item], item, block),
+            dst_ref=rows(outs[item], item, block),
+            send_sem=send_sem.at[item, block, way],
+            recv_sem=recv_sem.at[item, block],
+            device_id=(target, slab),
+            device_id_type=pl.DeviceIdType.MESH,
+        )
+
+    def side(block, way, mine=False):
+        return pltpu.make_async_remote_copy(
+            src_ref=ins[0] if mine else rows(outs[0], 0, block),
+            dst_ref=rows((prev_ref, next_ref)[way], 0, block),
+            send_sem=halo_send.at[block, way],
+            recv_sem=halo_recv.at[block, way],
+            device_id=(me, (after, before)[way]),
+            device_id_type=pl.DeviceIdType.MESH,
+        )
+
+    def sides(block, mine=False):
+        side(block, 0, mine).start()
+        side(block, 1, mine).start()
+
+    for item in range(3):
+        @pl.when(at < line - 1)
+        def _():
+            hop(item, me, 0, me + 2, True).start()
+
+        @pl.when(at > 0)
+        def _():
+            hop(item, me, 1, me - 2, True).start()
+
+        hop(item, me, 2, mate, True).start()
+    sides(me, True)
+    local = [
+        pltpu.make_async_copy(ins[item], rows(outs[item], item, me), local_sem.at[item])
+        for item in range(3)
+    ]
+    for copy in local:
+        copy.start()
+
+    def landed(item, block):
+        hop(item, block, 2, mate).wait_recv()
+
+    def from_mate(block):
+        for item in range(3):
+            landed(item, block)
+            if item == 0:
+                sides(block)
+
+    for step in range(1, line):
+        low, high = me - 2 * step, me + 2 * step
+
+        @pl.when(low >= 0)
+        def _():
+            for item in range(3):
+                landed(item, low)
+
+                @pl.when(at < line - 1)
+                def _():
+                    hop(item, low, 0, me + 2).start()
+
+                hop(item, low, 2, mate).start()
+                if item == 0:
+                    sides(low)
+
+        @pl.when(high < member_n)
+        def _():
+            for item in range(3):
+                landed(item, high)
+
+                @pl.when(at > 0)
+                def _():
+                    hop(item, high, 1, me - 2).start()
+
+                hop(item, high, 2, mate).start()
+                if item == 0:
+                    sides(high)
+
+        if step == 1:
+            from_mate(mate)
+        else:
+            @pl.when(mate - 2 * (step - 1) >= 0)
+            def _():
+                from_mate(mate - 2 * (step - 1))
+
+            @pl.when(mate + 2 * (step - 1) < member_n)
+            def _():
+                from_mate(mate + 2 * (step - 1))
+
+    @pl.when(mate - 2 * (line - 1) >= 0)
+    def _():
+        from_mate(mate - 2 * (line - 1))
+
+    @pl.when(mate + 2 * (line - 1) < member_n)
+    def _():
+        from_mate(mate + 2 * (line - 1))
+
+    for copy in local:
+        copy.wait()
+    for block in range(member_n):
+        for way in range(2):
+            side(block, way).wait()
+        place, same = block // 2, block % 2 == lane
+        for item in range(3):
+            @pl.when(same & (place <= at) & (at < line - 1))
+            def _():
+                hop(item, block, 0, mate).wait_send()
+
+            @pl.when(same & (place >= at) & (at > 0))
+            def _():
+                hop(item, block, 1, mate).wait_send()
+
+            @pl.when(same)
+            def _():
+                hop(item, block, 2, mate).wait_send()
+
+
+def gather(observed, picked, ints):
+    member_n, space_n = lax.axis_size("member"), lax.axis_size("space")
+    parts = (observed, picked, ints)
+    out = [jax.ShapeDtypeStruct((member_n * a.shape[0], a.shape[1]), a.dtype) for a in parts]
+    return pl.pallas_call(
+        functools.partial(gather_kernel, member_n, space_n),
+        out_shape=out + [out[0], out[0]],
+        in_specs=[pl.BlockSpec(memory_space=pltpu.VMEM)] * 3,
+        out_specs=[pl.BlockSpec(memory_space=pl.ANY)] * 5,
+        scratch_shapes=[
+            pltpu.SemaphoreType.DMA((3, member_n, 3)),
+            pltpu.SemaphoreType.DMA((3, member_n)),
+            pltpu.SemaphoreType.DMA((member_n, 2)),
+            pltpu.SemaphoreType.DMA((member_n, 2)),
+            pltpu.SemaphoreType.DMA((3,)),
+        ],
+        compiler_params=pltpu.CompilerParams(collective_id=0, has_side_effects=True),
+    )(*parts)
 
 
 def window_values(flat_row, width):
@@ -174,27 +337,26 @@
     ).reshape(share, obs_w)
     second = jnp.concatenate(pick(1), axis=1)
     ints = jnp.stack([loc_obs[0, 0], loc_tile[0, 0]]).astype(jnp.float32).reshape(-1)
-    extra = -(-ints.shape[0] // (2 * obs_w * 8)) * 8
-    ints = jnp.pad(ints, (0, extra * 2 * obs_w - ints.shape[0])).reshape(extra, 2 * obs_w)
-    sent = jnp.concatenate([jnp.concatenate([observed, second], axis=1), ints], axis=0)
-    got = lax.all_gather(sent, "member", axis=0)
-    own = got[:, :share, :obs_w].reshape(member_n * share, obs_w)
-    picked = got[:, :share, obs_w:].reshape(member_n * share, obs_w)
-    table = got[:, share:].reshape(member_n, -1)[:, : 2 * nb * loc]
+    extra = -(-ints.shape[0] // (8 * BLK)) * 8
+    ints = jnp.pad(ints, (0, extra * BLK - ints.shape[0])).reshape(extra, BLK)
+    cells = lax.all_to_all(states, "member", split_axis=1, concat_axis=0, tiled=True)
+    own, picked, table, before, after = gather(observed, second, ints)
+    table = table.reshape(member_n, extra * BLK)[:, : 2 * nb * loc]
     table = table.reshape(member_n, 2, nb, loc).astype(jnp.int32)
     table = table.transpose(1, 0, 2, 3).reshape(2, member_n * nb, loc)
     late = table[:, obs_cell[1, 0]]
-    reach = jnp.concatenate([loc_obs[0, 0], late[0]], axis=0)
-    tile_pick = jnp.concatenate([loc_tile[0, 0], late[1]], axis=0)
-
-    cells = lax.all_to_all(states, "member", split_axis=1, concat_axis=0, tiled=True)
-    cells, observed = update_cells(
-        cells, halo(own), window_values(obs_values[0], obs_w), window_values(obs_weights[0], obs_w),
-        loc_tiles, reach, tile_pick, picked, op_table, op_select[1, 0],
-    )
-    (cells,) = update_cells(
-        cells, halo(observed), window_values(obs_values[1], obs_w),
-        window_values(obs_weights[1], obs_w), loc_tiles, loc_obs[1, 0], loc_tile[1, 0],
+
+    values = [window_values(obs_values[b], obs_w) for b in range(2)]
+    weights = [window_values(obs_weights[b], obs_w) for b in range(2)]
+    window = (before, own, after)
+    observed = update_cells(
+        picked, window, values[0], weights[0], loc_tiles, late[0], late[1], op_table, op_select[1, 0]
+    )
+    cells = update_cells(
+        cells, window, values[0], weights[0], loc_tiles, loc_obs[0, 0], loc_tile[0, 0]
+    )
+    cells = update_cells(
+        cells, halo(observed), values[1], weights[1], loc_tiles, loc_obs[1, 0], loc_tile[1, 0]
     )
     return lax.all_to_all(cells, "member", split_axis=0, concat_axis=1, tiled=True)
 

time: 411 us -> 309 us (0.75)
  waiting for transfers between devices: 211 us -> 14.7 us
  Pallas kernels: 64.4 us -> 172 us
  between operations: 18.6 us -> 5.41 us
    all_gather x1 -> x0, waiting for transfers between devices: 127 us -> none  [per_device(): got = lax.all_gather(sent, 'member', axis=0)]
    pallas_call x2 -> x4, Pallas kernels: 64.4 us -> 172 us  [the longest x1 94.3 us: gather(): pl.pallas_call(functools.partial(gather_kernel, member_n, space_n), out_s...]
    ppermute x2 -> x1, waiting for transfers between devices: 82.9 us -> 11.9 us  [halo(): lax.ppermute(own, 'space', down)]
    slice x4 -> x2, local copies, waits for them, and re-layouts: 5.75 us -> 0.67 us  [the longest x1 0.59 us: per_device(): late[1]]
  transfers between devices with their start and end apart: 6 -> 3, of which waited for: 5 -> 2; matrix products, arithmetic and copies ran while one was open for 4% -> 7% of each run, Pallas kernels for 0% -> 47%
where the time goes in v2:
time: 309 us; the launch traced here: 308 us
  Pallas kernels  172 us (56%)
  blocking collectives  77.1 us (25%)
  local copies, waits for them, and re-layouts  26 us (8%)
  waiting for transfers between devices  14.7 us (5%)
  starting transfers between devices  9.31 us (3%)
  between operations  5.41 us (2%)
    pallas_call x1, Pallas kernels, gather(): pl.pallas_call(functools.partial(gather_kernel, member_n, space_n), out_s...  94.3 us
    pallas_call x3, Pallas kernels, update_cells(): pl.pallas_call(functools.partial(update_kernel, ob, loc, picks), grid_spe...  77.3 us
    all_to_all x1, blocking collectives, per_device(): lax.all_to_all(cells, 'member', split_axis=0, concat_axis=1, tiled=True)  77.1 us
    ppermute x1, waiting for transfers between devices, halo(): lax.ppermute(own, 'space', down)  11.9 us
    all_to_all x1, starting transfers between devices, per_device(): lax.all_to_all(states, 'member', split_axis=1, concat_axis=0, tiled=True)  7.42 us
  transfers between devices with their start and end apart: 3, of which 2 were waited for; matrix products, arithmetic and copies ran while one was open for 7% of the time, Pallas kernels for 47%

profile of v2, /device:TPU:0, one launch (start us, length us, event | category | flops | bytes accessed | tf_op | source)
XLA Modules:
  0.0 308.1 jit_solution(5603776333594277989)
XLA Ops:
  0.0 3.8 %copy.42 = f32[16,8,8,768]{3,2,0,1:T(8,128)} copy(f32[16,8,8,768]{3,2,1,0:T(8,128)} %bitcast.63) | data formatting | bytes 6291456 | tf_op jit(solution)/shard_map/all_to_all | solution.py:342
  3.9 7.4 %all-to-all-start = ((f32[128,8,768]{2,0,1:T(8,128)}), f32[128,8,768]{2,0,1:T(8,128)S(1)}, u32[]{:S(2)}, u32[]{:S(2)}) async-start(f32[128,8,768]{2,0,1:T(8,128)} %bitcast.61), calls=%async_computation | async-start | bytes 6291456 | tf_op jit(solution)/shard_map/all_to_all | solution.py:342
  11.3 0.7 fusion.14
  17.3 0.6 slice_bitcast_fusion.2
  17.9 0.6 slice_bitcast_fusion.1
  18.5 0.7 convert_element_type.16
  19.9 0.6 reshape.159.refs_8_.refs_9_
  21.1 0.6 reshape.158.refs_7_.refs_8_
  22.2 1.6 gather_fusion
  23.8 1.8 constant_dynamic-slice_fusion.3
  25.6 1.4 fusion
  26.9 1.8 copy.28.refs_0_
  28.7 1.3 pad_bitcast_fusion.refs_2_
  30.0 1.6 pad_maximum_fusion.refs_1_
  31.6 94.3 %shard_map.91 = (f32[1024,512]{1,0:T(8,128)}, f32[1024,512]{1,0:T(8,128)}, f32[64,128]{1,0:T(8,128)}, f32[1024,512]{1,0:T(8,128)}, f32[1024,512]{1,0:T(8,128)}) custom-call(f32[128,512]{1,0:T(8,128)} %copy.28.refs_0_, f32[128,512]{1,0:T(8,128)} %pad_maximum_fusion.refs_1_, f32[8,128]{1,0:T(8,128)} %pad_bitcast_fusion.refs_2_), custom_call_target="tpu_custom_call" | custom-call | tf_op jit(solution)/shard_map/pallas_call | solution.py:289
  125.9 0.8 reshape.160
  127.9 1.1 slice_bitcast_fusion.refs_2_
  129.7 21.4 %shard_map.93.refs_5_ = f32[1024,512]{1,0:T(8,128)} custom-call(s32[4,8]{1,0:T(4,128)} %bitcast.71, s32[4,8]{1,0:T(4,128)} %bitcast.70, s32[4]{0:T(128)} %slice_bitcast_fusion.refs_2_, f32[1024,512]{1,0:T(8,128)} %get-tuple-element.14.refs_3_, f32[8,128,128]{2,1,0:T(8,128)} %refs_4_.1, f32[1024,512]{1,0:T(8,128)} %get-tuple-element.10.refs_4_.refs_5_, ...), custom_call_target="tpu_custom_call" | custom-call | flops 8589934592 | bytes 33554432 | tf_op jit(solution)/shard_map/pallas_call | solution.py:103
  151.0 1.9 collective-permute-start.1
  152.9 0.7 gather_fusion.5
  153.6 0.6 reshape.163.refs_8_
  154.2 0.7 gather_fusion.4
  154.9 0.6 reshape.162.refs_7_
  156.1 0.6 copy_bitcast_fusion.1
  156.7 0.6 broadcast_11_refs_2_.2.refs_2_
  157.4 1.1 copy-done
  158.4 28.0 %shard_map.92.refs_3_ = f32[1024,768]{1,0:T(8,128)} custom-call(s32[6,8]{1,0:T(8,128)} %get-tuple-element.47.refs_0_, s32[6,8]{1,0:T(8,128)} %get-tuple-element.45.refs_1_, s32[4]{0:T(128)} %broadcast_11_refs_2_.2.refs_2_, f32[1024,768]{1,0:T(8,128)} %bitcast.64, f32[1024,512]{1,0:T(8,128)} %get-tuple-element.10.refs_4_.refs_5_, ...), custom_call_target="tpu_custom_call" | custom-call | flops 12884901888 | bytes 33554432 | tf_op jit(solution)/shard_map/pallas_call | solution.py:103
  186.4 11.9 %collective-permute-done.1.refs_6_ = f32[1024,512]{1,0:T(8,128)} collective-permute-done((f32[1024,512]{1,0:T(8,128)}, f32[1024,512]{1,0:T(8,128)}, u32[]{:S(2)}, u32[]{:S(2)}) %collective-permute-start.1) | collective-permute-done | bytes 2097184 | tf_op jit(solution)/shard_map/ppermute | solution.py:316
  198.3 2.8 collective-permute-done.refs_4_
  201.1 27.9 %shard_map.94 = f32[1024,768]{1,0:T(8,128)} custom-call(s32[6,8]{1,0:T(8,128)} %get-tuple-element.48.refs_0_, s32[6,8]{1,0:T(8,128)} %get-tuple-element.46.refs_1_, s32[4]{0:T(128)} %broadcast_11_refs_2_.2.refs_2_, f32[1024,768]{1,0:T(8,128)} %shard_map.92.refs_3_, f32[1024,512]{1,0:T(8,128)} %collective-permute-done.refs_4_, ...), custom_call_target="tpu_custom_call" | custom-call | flops 12884901888 | bytes 33554432 | tf_op jit(solution)/shard_map/pallas_call | solution.py:103
  229.0 77.1 %all_to_all.38 = f32[8,128,768]{2,1,0:T(8,128)S(1)} all-to-all(f32[8,128,768]{2,1,0:T(8,128)} %bitcast.65), channel_id=1, replica_groups=mesh['member'=8,'space'=4] {'member'}, dimensions={0} | all-to-all | bytes 6291456 | tf_op jit(solution)/shard_map/all_to_all | solution.py:361
  306.1 2.0 copy.36
  (45 shorter events, 4.3 us)
Async XLA Ops:
  3.9 7.5 %copy-start.1 = (s32[2,1,4]{2,1,0:T(1,128)S(1)}, s32[2,1,4]{2,1,0:T(1,128)}, u32[]{:S(2)}) copy-start(s32[2,1,4]{2,1,0:T(1,128)} %param.12) | copy-start | bytes 100
  3.9 13.4 %copy-start.9 = (s32[2,1,6,8]{3,1,2,0:T(1,128)S(1)}, s32[2,1,6,8]{3,1,2,0:T(1,128)}, u32[]{:S(2)}) copy-start(s32[2,1,6,8]{3,1,2,0:T(1,128)} %param.15) | copy-start | bytes 1156
  3.9 14.0 %copy-start.10 = (s32[2,1,6,8]{3,1,2,0:T(1,128)S(1)}, s32[2,1,6,8]{3,1,2,0:T(1,128)}, u32[]{:S(2)}) copy-start(s32[2,1,6,8]{3,1,2,0:T(1,128)} %param.16) | copy-start | bytes 1156
  3.9 15.3 %copy-start.2 = (f32[2,2048]{1,0:T(2,128)S(1)}, f32[2,2048]{1,0:T(2,128)}, u32[]{:S(2)}) copy-start(f32[2,2048]{1,0:T(2,128)} %param.11) | copy-start | bytes 49156
  3.9 15.3 %copy-start.3 = (f32[2,2048]{1,0:T(2,128)S(1)}, f32[2,2048]{1,0:T(2,128)}, u32[]{:S(2)}) copy-start(f32[2,2048]{1,0:T(2,128)} %param.10) | copy-start | bytes 49156
  3.9 17.8 %copy-start.11 = (s32[2,1,4]{2,1,0:T(1,128)S(1)}, s32[2,1,4]{2,1,0:T(1,128)}, u32[]{:S(2)}) copy-start(s32[2,1,4]{2,1,0:T(1,128)} %param.13) | copy-start | bytes 100
  3.9 152.9 %all-to-all-start = ((f32[128,8,768]{2,0,1:T(8,128)}), f32[128,8,768]{2,0,1:T(8,128)S(1)}, u32[]{:S(2)}, u32[]{:S(2)}) async-start(f32[128,8,768]{2,0,1:T(8,128)} %bitcast.61), calls=%async_computation | async-start | bytes 6291456 | tf_op jit(solution)/shard_map/all_to_all | solution.py:342
  19.3 2.9 copy-start.8
  129.7 25.9 %copy-start.6 = (s32[1,1,6,8]{3,1,2,0:T(1,128)S(1)}, s32[1,1,6,8]{3,1,2,0:T(1,128)}, u32[]{:S(2)}) copy-start(s32[1,1,6,8]{3,1,2,0:T(1,128)} %get-tuple-element.28) | copy-start | bytes 580
  129.7 25.9 %copy-start.7 = (s32[1,1,6,8]{3,1,2,0:T(1,128)S(1)}, s32[1,1,6,8]{3,1,2,0:T(1,128)}, u32[]{:S(2)}) copy-start(s32[1,1,6,8]{3,1,2,0:T(1,128)} %get-tuple-element.29) | copy-start | bytes 580
  129.7 26.5 %copy-start.4 = (s32[1,1,6,8]{3,1,2,0:T(1,128)S(1)}, s32[1,1,6,8]{3,1,2,0:T(1,128)}, u32[]{:S(2)}) copy-start(s32[1,1,6,8]{3,1,2,0:T(1,128)} %get-tuple-element.31) | copy-start | bytes 580
  129.7 26.5 %copy-start.5 = (s32[1,1,6,8]{3,1,2,0:T(1,128)S(1)}, s32[1,1,6,8]{3,1,2,0:T(1,128)}, u32[]{:S(2)}) copy-start(s32[1,1,6,8]{3,1,2,0:T(1,128)} %get-tuple-element.32) | copy-start | bytes 580
  151.0 47.3 %collective-permute-start.1 = (f32[1024,512]{1,0:T(8,128)}, f32[1024,512]{1,0:T(8,128)}, u32[]{:S(2)}, u32[]{:S(2)}) collective-permute-start(f32[1024,512]{1,0:T(8,128)} %shard_map.93.refs_5_), channel_id=1, source_target_pairs={{1,0},{2,1},{3,2},{0,3},{5,4},{6,5},{7,6},{4,7},{9,8},{10,9},{11,1... | collective-permute-start | bytes 6291464 | tf_op jit(solution)/shard_map/ppermute | solution.py:316
  152.9 48.2 %collective-permute-start = (f32[1024,512]{1,0:T(8,128)}, f32[1024,512]{1,0:T(8,128)}, u32[]{:S(2)}, u32[]{:S(2)}) collective-permute-start(f32[1024,512]{1,0:T(8,128)} %shard_map.93.refs_5_), channel_id=1, source_target_pairs={{0,1},{1,2},{2,3},{3,0},{4,5},{5,6},{6,7},{7,4},{8,9},{9,10},{10,1... | collective-permute-start | bytes 6291464 | tf_op jit(solution)/shard_map/ppermute | solution.py:316
  156.7 1.7 copy-start

commit v3 on v2

v3 whole, which is shorter than its diff:
```python
import functools

import jax
import jax.numpy as jnp
from jax import lax
from jax.experimental import pallas as pl
from jax.experimental.pallas import tpu as pltpu
from jax.sharding import PartitionSpec as P

BLK = 128
NT_DIMS = (((1,), (1,)), ((), ()))


def split(x):
    hi = x.astype(jnp.bfloat16)
    lo = (x - hi.astype(jnp.float32)).astype(jnp.bfloat16)
    return hi, lo


def dot(a, b):
    return jnp.dot(a, b, preferred_element_type=jnp.float32)


def dot_nt(a, b):
    return lax.dot_general(a, b, NT_DIMS, preferred_element_type=jnp.float32)


def send(src, dst, send_sem, recv_sem, member, space):
    return pltpu.make_async_remote_copy(
        src_ref=src,
        dst_ref=dst,
        send_sem=send_sem,
        recv_sem=recv_sem,
        device_id=(member, space),
        device_id_type=pl.DeviceIdType.MESH,
    )


def columns(ref, block):
    return ref.at[:, pl.ds(pl.multiple_of(block * BLK, BLK), BLK)]


def ring_of_slabs(space_n):
    slab = lax.axis_index("space")
    return slab, lax.rem(slab + 1, space_n), lax.rem(slab + space_n - 1, space_n)


def load_window(batch_no, ob, space_n, window, values_ref, weights_ref, scratch):
    hi_ref, lo_ref, d_ref, w_ref = scratch[:4]
    members = window[0].shape[0]
    slab = lax.axis_index("space")
    for place, ref in enumerate(window):
        source = lax.rem(slab + space_n - 1 + place, space_n)
        for o in range(ob):
            j = place * ob + o
            row = (batch_no * space_n + source) * ob + o
            block = ref[:, o * BLK:(o + 1) * BLK]
            mean = jnp.sum(block, axis=0, keepdims=True) * (1.0 / members)
            hi, lo = split(block - mean)
            hi_ref[j] = hi
            lo_ref[j] = lo
            w_ref[j] = weights_ref[row]
            d_ref[j] = weights_ref[row] * (values_ref[row] - mean)


def update(cell, picks, tiles_ref, scratch):
    hi_ref, lo_ref, d_ref, w_ref, acc_ref = scratch
    members = cell.shape[0]
    mean = jnp.sum(cell, axis=0, keepdims=True) * (1.0 / members)
    hi, lo = split(jnp.transpose(cell - mean))
    both = jnp.concatenate([hi, lo], axis=0)
    ones = []
    for pair in range(len(picks) // 2):
        (first, tile_a), (second, tile_b) = picks[2 * pair], picks[2 * pair + 1]
        obs_hi = jnp.concatenate([hi_ref[first], hi_ref[second]], axis=1)
        obs_lo = jnp.concatenate([lo_ref[first], lo_ref[second]], axis=1)
        part = dot(both, obs_hi)
        cov = part[:BLK] + part[BLK:] + dot(hi, obs_lo)
        tile = jnp.concatenate([tiles_ref[tile_a], tiles_ref[tile_b]], axis=1)
        gain = tile * (cov * (1.0 / (members - 1)))
        d = jnp.concatenate([d_ref[first], d_ref[second]], axis=1)
        w = jnp.concatenate([w_ref[first], w_ref[second]], axis=1)
        ones.append(jnp.sum(gain * d, axis=1, keepdims=True))
        gain_hi, gain_lo = split(gain * (-0.5 * w))
        step = dot_nt(obs_hi, jnp.concatenate([gain_hi, gain_lo], axis=0))
        step = step[:, :BLK] + step[:, BLK:] + dot_nt(obs_lo, gain_hi)
        if pair == 0:
            acc_ref[...] = step
        else:
            acc_ref[...] += step
    shift = functools.reduce(jnp.add, ones)
    row = jnp.transpose(jnp.broadcast_to(shift, (BLK, BLK)))[:1]
    return cell + (acc_ref[...] + row)


def window_scratch(ob, members):
    return [
        pltpu.VMEM((3 * ob, members, BLK), jnp.bfloat16),
        pltpu.VMEM((3 * ob, members, BLK), jnp.bfloat16),
        pltpu.VMEM((3 * ob, 1, BLK), jnp.float32),
        pltpu.VMEM((3 * ob, 1, BLK), jnp.float32),
        pltpu.VMEM((members, BLK), jnp.float32),
    ]


def params(collective_id):
    return pltpu.CompilerParams(
        dimension_semantics=("arbitrary",),
        vmem_limit_bytes=56 * 1024 * 1024,
        collective_id=collective_id,
        has_side_effects=True,
    )


def cost(blocks, members, loc):
    return pl.CostEstimate(
        flops=16 * blocks * members * BLK * BLK * loc, bytes_accessed=32 << 20, transcendentals=0
    )


def first_kernel(nb, ob, loc, space_n, *refs):
    ints_ref, cell_ref, op_ref, reach_ref, tile_ref, picked_ref, cells_ref, table_ref = refs[:8]
    before_ref, own_ref, after_ref, values_ref, weights_ref, tiles_ref = refs[8:14]
    out_ref, obs_ref, prev_ref, next_ref = refs[14:18]
    scratch, (stage_ref, send_sem, recv_sem) = refs[18:23], refs[23:]
    n = pl.program_id(0)
    me = lax.axis_index("member")
    slab, after, before = ring_of_slabs(space_n)
    per_member = -(-2 * nb * loc // (8 * BLK)) * 8

    def side(block, way):
        return send(
            stage_ref.at[block],
            columns((prev_ref, next_ref)[way], block),
            send_sem.at[block, way],
            recv_sem.at[block, way],
            me,
            (after, before)[way],
        )

    @pl.when(n == 0)
    def _():
        barrier = pltpu.get_barrier_semaphore()
        for space in (after, before):
            pl.semaphore_signal(
                barrier, inc=1, device_id=(me, space), device_id_type=pl.DeviceIdType.MESH
            )
        pl.semaphore_wait(barrier, 2)
        load_window(0, ob, space_n, (before_ref, own_ref, after_ref), values_ref, weights_ref, scratch)

    @pl.when(n < ob)
    def _():
        cell = cell_ref[ob + n]
        owner = cell // nb

        def look(which, l):
            at = (which * nb + cell - owner * nb) * loc + l
            return ints_ref[owner * per_member + at // BLK, lax.rem(at, BLK)]

        picks = [(look(0, l), look(1, l)) for l in range(loc)]
        fresh_hi, fresh_lo = split(update(picked_ref[...], picks, tiles_ref, scratch))
        op_hi, op_lo = split(table_ref[op_ref[ob + n]])
        part = dot_nt(fresh_hi, jnp.concatenate([op_hi, op_lo], axis=0))
        part = part[:, :BLK] + part[:, BLK:] + dot_nt(fresh_lo, op_hi)
        obs_ref[...] = part
        stage_ref[n] = part
        side(n, 0).start()
        side(n, 1).start()

    @pl.when(n >= ob)
    def _():
        b = jnp.maximum(n - ob, 0)
        picks = [(reach_ref[b, l], tile_ref[b, l]) for l in range(loc)]
        out_ref[...] = update(cells_ref[...], picks, tiles_ref, scratch)

    @pl.when(n == ob + nb - 1)
    def _():
        for block in range(ob):
            side(block, 0).wait()
            side(block, 1).wait()


def first_batch(ints, cell, ops, reach, tile_pick, picked, cells, table, window, values, weights, tiles):
    members, wide = picked.shape
    nb, ob, loc = cells.shape[1] // BLK, wide // BLK, reach.shape[1]
    whole = pl.BlockSpec(memory_space=pltpu.VMEM)
    anywhere = pl.BlockSpec(memory_space=pl.ANY)
    early = pl.BlockSpec((members, BLK), lambda n, *_: (0, jnp.minimum(n, ob - 1)))
    late = pl.BlockSpec((members, BLK), lambda n, *_: (0, jnp.maximum(n - ob, 0)))
    seen = jax.ShapeDtypeStruct(picked.shape, jnp.float32)
    return pl.pallas_call(
        functools.partial(first_kernel, nb, ob, loc, lax.axis_size("space")),
        grid_spec=pltpu.PrefetchScalarGridSpec(
            num_scalar_prefetch=5,
            grid=(ob + nb,),
            in_specs=[early, late] + [whole] * 7,
            out_specs=[late, early, anywhere, anywhere],
            scratch_shapes=window_scratch(ob, members) + [
                pltpu.VMEM((ob, members, BLK), jnp.float32),
                pltpu.SemaphoreType.DMA((ob, 2)),
                pltpu.SemaphoreType.DMA((ob, 2)),
            ],
        ),
        out_shape=[jax.ShapeDtypeStruct(cells.shape, jnp.float32), seen, seen, seen],
        compiler_params=params(1),
        cost_estimate=cost(ob + nb, members, loc),
    )(ints, cell, ops, reach, tile_pick, picked, cells, table, *window, values, weights, tiles)


def last_kernel(nb, ob, loc, member_n, space_n, *refs):
    reach_ref, tile_ref, cells_ref, before_ref, own_ref, after_ref = refs[:6]
    values_ref, weights_ref, tiles_ref, out_ref = refs[6:10]
    scratch, (stage_ref, send_sem, recv_sem, local_sem) = refs[10:15], refs[15:]
    n = pl.program_id(0)
    me = lax.axis_index("member")
    slab = lax.axis_index("space")
    share = out_ref.shape[0]

    def part(block, member):
        return stage_ref.at[block, pl.ds(pl.multiple_of(member * share, 8), share)]

    def give(block, hop):
        peer = lax.rem(me + hop, member_n)
        return send(
            part(block, peer),
            columns(out_ref, me * nb + block),
            send_sem.at[block, hop],
            recv_sem.at[block, me],
            peer,
            slab,
        )

    def keep(block):
        return pltpu.make_async_copy(
            part(block, me), columns(out_ref, me * nb + block), local_sem.at[block]
        )

    @pl.when(n == 0)
    def _():
        barrier = pltpu.get_barrier_semaphore()
        for hop in range(1, member_n):
            peer = lax.rem(me + hop, member_n)
            pl.semaphore_signal(
                barrier, inc=1, device_id=(peer, slab), device_id_type=pl.DeviceIdType.MESH
            )
        pl.semaphore_wait(barrier, member_n - 1)
        load_window(1, ob, space_n, (before_ref, own_ref, after_ref), values_ref, weights_ref, scratch)

    picks = [(reach_ref[n, l], tile_ref[n, l]) for l in range(loc)]
    stage_ref[n] = update(cells_ref[...], picks, tiles_ref, scratch)
    for hop in range(1, member_n):
        give(n, hop).start()
    keep(n).start()

    @pl.when(n == nb - 1)
    def _():
        for block in range(nb):
            keep(block).wait()
            for hop in range(1, member_n):
                give(block, hop).wait_send()
                peer = lax.rem(me + hop, member_n)
                send(
                    part(block, peer),
                    columns(out_ref, peer * nb + block),
                    send_sem.at[block, hop],
                    recv_sem.at[block, peer],
                    peer,
                    slab,
                ).wait_recv()


def last_batch(reach, tile_pick, cells, window, values, weights, tiles):
    members, width = cells.shape
    nb, ob, loc = width // BLK, window[0].shape[1] // BLK, reach.shape[1]
    member_n = lax.axis_size("member")
    whole = pl.BlockSpec(memory_space=pltpu.VMEM)
    block = pl.BlockSpec((members, BLK), lambda n, *_: (0, n))
    return pl.pallas_call(
        functools.partial(last_kernel, nb, ob, loc, member_n, lax.axis_size("space")),
        grid_spec=pltpu.PrefetchScalarGridSpec(
            num_scalar_prefetch=2,
            grid=(nb,),
            in_specs=[block] + [whole] * 6,
            out_specs=pl.BlockSpec(memory_space=pl.ANY),
            scratch_shapes=window_scratch(ob, members) + [
                pltpu.VMEM((nb, members, BLK), jnp.float32),
                pltpu.SemaphoreType.DMA((nb, member_n)),
                pltpu.SemaphoreType.DMA((nb, member_n)),
                pltpu.SemaphoreType.DMA((nb,)),
            ],
        ),
        out_shape=jax.ShapeDtypeStruct((members // member_n, width * member_n), jnp.float32),
        compiler_params=params(2),
        cost_estimate=cost(nb, members, loc),
    )(reach, tile_pick, cells, *window, values, weights, tiles)


def pick_kernel(ob, cell_ref, op_ref, states_ref, op_block_ref, observed_ref, picked_ref):
    n = pl.program_id(0)

    @pl.when(n < ob)
    def _():
        observed_ref[...] = lax.dot_general(
            states_ref[...],
            op_block_ref[0],
            NT_DIMS,
            precision=lax.Precision.HIGHEST,
            preferred_element_type=jnp.float32,
        )

    @pl.when(n >= ob)
    def _():
        picked_ref[...] = states_ref[...]


def pick_blocks(cell, ops, states, table):
    share, ob = states.shape[0], cell.shape[0] // 2
    out = jax.ShapeDtypeStruct((share, ob * BLK), jnp.float32)
    return pl.pallas_call(
        functools.partial(pick_kernel, ob),
        grid_spec=pltpu.PrefetchScalarGridSpec(
            num_scalar_prefetch=2,
            grid=(2 * ob,),
            in_specs=[
                pl.BlockSpec((share, BLK), lambda n, cell, ops: (0, cell[n])),
                pl.BlockSpec((1, BLK, BLK), lambda n, cell, ops: (ops[n], 0, 0)),
            ],
            out_specs=[
                pl.BlockSpec((share, BLK), lambda n, *_: (0, jnp.minimum(n, ob - 1))),
                pl.BlockSpec((share, BLK), lambda n, *_: (0, jnp.maximum(n - ob, 0))),
            ],
        ),
        out_shape=[out, out],
    )(cell, ops, states, table)


def gather_kernel(member_n, space_n, *refs):
    ins, refs = refs[:3], refs[3:]
    outs, refs = refs[:3], refs[3:]
    prev_ref, next_ref, send_sem, recv_sem, halo_send, halo_recv, local_sem = refs
    me = lax.axis_index("member")
    slab = lax.axis_index("space")
    line = member_n // 2
    at, lane = me // 2, lax.rem(me, 2)
    mate = at * 2 + 1 - lane
    after = lax.rem(slab + 1, space_n)
    before = lax.rem(slab + space_n - 1, space_n)

    barrier = pltpu.get_barrier_semaphore()

    def greet(member, space):
        pl.semaphore_signal(
            barrier, inc=1, device_id=(member, space), device_id_type=pl.DeviceIdType.MESH
        )

    greet(mate, slab)
    greet(me, after)
    greet(me, before)

    @pl.when(at > 0)
    def _():
        greet(me - 2, slab)

    @pl.when(at < line - 1)
    def _():
        greet(me + 2, slab)

    pl.semaphore_wait(
        barrier, 3 + jnp.where(at > 0, 1, 0) + jnp.where(at < line - 1, 1, 0)
    )

    def rows(ref, item, block):
        size = ins[item].shape[0]
        return ref.at[pl.ds(pl.multiple_of(block * size, 8), size)]

    def hop(item, block, way, target, mine=False):
        return pltpu.make_async_remote_copy(
            src_ref=ins[item] if mine else rows(outs[item], item, block),
            dst_ref=rows(outs[item], item, block),
            send_sem=send_sem.at[item, block, way],
            recv_sem=recv_sem.at[item, block],
            device_id=(target, slab),
            device_id_type=pl.DeviceIdType.MESH,
        )

    def side(block, way, mine=False):
        return pltpu.make_async_remote_copy(
            src_ref=ins[0] if mine else rows(outs[0], 0, block),
            dst_ref=rows((prev_ref, next_ref)[way], 0, block),
            send_sem=halo_send.at[block, way],
            recv_sem=halo_recv.at[block, way],
            device_id=(me, (after, before)[way]),
            device_id_type=pl.DeviceIdType.MESH,
        )

    def sides(block, mine=False):
        side(block, 0, mine).start()
        side(block, 1, mine).start()

    for item in range(3):
        @pl.when(at < line - 1)
        def _():
            hop(item, me, 0, me + 2, True).start()

        @pl.when(at > 0)
        def _():
            hop(item, me, 1, me - 2, True).start()

        hop(item, me, 2, mate, True).start()
    sides(me, True)
    local = [
        pltpu.make_async_copy(ins[item], rows(outs[item], item, me), local_sem.at[item])
        for item in range(3)
    ]
    for copy in local:
        copy.start()

    def landed(item, block):
        hop(item, block, 2, mate).wait_recv()

    def from_mate(block):
        for item in range(3):
            landed(item, block)
            if item == 0:
                sides(block)

    for step in range(1, line):
        low, high = me - 2 * step, me + 2 * step

        @pl.when(low >= 0)
        def _():
            for item in range(3):
                landed(item, low)

                @pl.when(at < line - 1)
                def _():
                    hop(item, low, 0, me + 2).start()

                hop(item, low, 2, mate).start()
                if item == 0:
                    sides(low)

        @pl.when(high < member_n)
        def _():
            for item in range(3):
                landed(item, high)

                @pl.when(at > 0)
                def _():
                    hop(item, high, 1, me - 2).start()

                hop(item, high, 2, mate).start()
                if item == 0:
                    sides(high)

        if step == 1:
            from_mate(mate)
        else:
            @pl.when(mate - 2 * (step - 1) >= 0)
            def _():
                from_mate(mate - 2 * (step - 1))

            @pl.when(mate + 2 * (step - 1) < member_n)
            def _():
                from_mate(mate + 2 * (step - 1))

    @pl.when(mate - 2 * (line - 1) >= 0)
    def _():
        from_mate(mate - 2 * (line - 1))

    @pl.when(mate + 2 * (line - 1) < member_n)
    def _():
        from_mate(mate + 2 * (line - 1))

    for copy in local:
        copy.wait()
    for block in range(member_n):
        for way in range(2):
            side(block, way).wait()
        place, same = block // 2, block % 2 == lane
        for item in range(3):
            @pl.when(same & (place <= at) & (at < line - 1))
            def _():
                hop(item, block, 0, mate).wait_send()

            @pl.when(same & (place >= at) & (at > 0))
            def _():
                hop(item, block, 1, mate).wait_send()

            @pl.when(same)
            def _():
                hop(item, block, 2, mate).wait_send()


def gather(observed, picked, ints):
    member_n, space_n = lax.axis_size("member"), lax.axis_size("space")
    parts = (observed, picked, ints)
    out = [jax.ShapeDtypeStruct((member_n * a.shape[0], a.shape[1]), a.dtype) for a in parts]
    return pl.pallas_call(
        functools.partial(gather_kernel, member_n, space_n),
        out_shape=out + [out[0], out[0]],
        in_specs=[pl.BlockSpec(memory_space=pltpu.VMEM)] * 3,
        out_specs=[pl.BlockSpec(memory_space=pl.ANY)] * 5,
        scratch_shapes=[
            pltpu.SemaphoreType.DMA((3, member_n, 3)),
            pltpu.SemaphoreType.DMA((3, member_n)),
            pltpu.SemaphoreType.DMA((member_n, 2)),
            pltpu.SemaphoreType.DMA((member_n, 2)),
            pltpu.SemaphoreType.DMA((3,)),
        ],
        compiler_params=pltpu.CompilerParams(collective_id=0, has_side_effects=True),
    )(*parts)


def per_device(
    states, obs_values, obs_weights, obs_cell, op_select, op_table, loc_obs, loc_tile, loc_tiles
):
    nb, loc = loc_obs.shape[2:]
    cell, ops = obs_cell.reshape(-1), op_select.reshape(-1)
    values = obs_values.reshape(-1, 1, BLK)
    weights = obs_weights.reshape(-1, 1, BLK)
    ints = jnp.concatenate([loc_obs[0, 0], loc_tile[0, 0]]).reshape(-1)
    extra = -(-ints.shape[0] // (8 * BLK)) * 8
    ints = jnp.pad(ints, (0, extra * BLK - ints.shape[0])).reshape(extra, BLK)

    cells = lax.all_to_all(states, "member", split_axis=1, concat_axis=0, tiled=True)
    observed, picked = pick_blocks(cell, ops, states, op_table)
    own, picked, ints, before, after = gather(observed, picked, ints)
    cells, own, before, after = first_batch(
        ints, cell, ops, loc_obs[0, 0], loc_tile[0, 0], picked, cells, op_table,
        (before, own, after), values, weights, loc_tiles,
    )
    return last_batch(
        loc_obs[1, 0], loc_tile[1, 0], cells, (before, own, after), values, weights, loc_tiles
    )


def solution(mesh):
    placed = (
        P("member", "space"),
        P(),
        P(),
        P(None, "space", None),
        P(None, "space", None),
        P(),
        P(None, "space", "member", None),
        P(None, "space", "member", None),
        P(),
    )
    return jax.shard_map(
        per_device, mesh=mesh, in_specs=placed, out_specs=P("member", "space"), check_vma=False
    )
```

time: 309 us -> 274 us (0.89)
  blocking collectives: 77.1 us -> 0 us
  Pallas kernels: 172 us -> 249 us
  waiting for transfers between devices: 14.7 us -> 0.01 us
  local copies, waits for them, and re-layouts: 26 us -> 14.2 us
  between operations: 5.41 us -> 0.1 us
    all_to_all x1 -> x0, blocking collectives: 77.1 us -> none  [per_device(): lax.all_to_all(cells, 'member', split_axis=0, concat_axis=1, tiled=True)]
    pallas_call x3, Pallas kernels: 77.3 us -> 147 us  [the longest x1 82.9 us: last_batch(): pl.pallas_call(functools.partial(last_kernel, nb, ob, loc, member_n, lax....]
    ppermute x2 -> x0, waiting for transfers between devices: 14.7 us -> none  [the longest x1 11.9 us: halo(): lax.ppermute(own, 'space', down)]
    pallas_call x1, Pallas kernels: 94.3 us -> 102 us  [gather(): pl.pallas_call(functools.partial(gather_kernel, member_n, space_n), out_s...]
    unnamed x24 -> x20, local copies, waits for them, and re-layouts: 1.11 us -> 6.08 us
    gather x6 -> x0, local copies, waits for them, and re-layouts: 4.66 us -> none  [the longest x4 2.49 us: window_values(): return by_slab[pick].reshape(3 * width // BLK, 1, BLK)]
  transfers between devices with their start and end apart: 3 -> 1, of which waited for: 2 -> 0; matrix products, arithmetic and copies ran while one was open for 7% -> 2% of each run, Pallas kernels for 47% -> 40%
where the time goes in v3:
time: 274 us; the launch traced here: 272 us
  Pallas kernels  249 us (91%)
  local copies, waits for them, and re-layouts  14.2 us (5%)
  starting transfers between devices  7.42 us (3%)
    pallas_call x1, Pallas kernels, gather(): pl.pallas_call(functools.partial(gather_kernel, member_n, space_n), out_s...  102 us
    pallas_call x1, Pallas kernels, last_batch(): pl.pallas_call(functools.partial(last_kernel, nb, ob, loc, member_n, lax....  82.9 us
    pallas_call x1, Pallas kernels, first_batch(): pl.pallas_call(functools.partial(first_kernel, nb, ob, loc, lax.axis_size...  57.9 us
    all_to_all x1, starting transfers between devices, per_device(): lax.all_to_all(states, 'member', split_axis=1, concat_axis=0, tiled=True)  7.42 us
    unnamed x20, local copies, waits for them, and re-layouts  6.08 us
    pallas_call x1, Pallas kernels, pick_blocks(): pl.pallas_call(functools.partial(pick_kernel, ob), grid_spec=pltpu.Prefet...  6.07 us
  transfers between devices with their start and end apart: 1, of which 0 were waited for; matrix products, arithmetic and copies ran while one was open for 2% of the time, Pallas kernels for 40%

profile of v3, /device:TPU:0, one launch (start us, length us, event | category | flops | bytes accessed | tf_op | source)
XLA Modules:
  0.0 272.3 jit_solution(8585753684881146515)
XLA Ops:
  0.0 3.8 %copy.30 = f32[16,8,8,768]{3,2,0,1:T(8,128)} copy(f32[16,8,8,768]{3,2,1,0:T(8,128)} %bitcast.17) | data formatting | bytes 6291456 | tf_op jit(solution)/shard_map/all_to_all | solution.py:526
  3.9 0.0 copy-start.7
  3.9 0.0 copy-start.1
  3.9 0.0 copy-start.2
  3.9 7.4 %all-to-all-start = ((f32[128,8,768]{2,0,1:T(8,128)}), f32[128,8,768]{2,0,1:T(8,128)S(1)}, u32[]{:S(2)}, u32[]{:S(2)}) async-start(f32[128,8,768]{2,0,1:T(8,128)} %bitcast.16), calls=%async_computation | async-start | bytes 6291456 | tf_op jit(solution)/shard_map/all_to_all | solution.py:526
  11.3 0.5 broadcast.8
  11.8 0.0 copy-done.7
  11.8 0.7 reduce.6
  12.5 0.6 reshape.21.cell_ref.refs_1_
  13.1 0.0 copy-done.8
  13.1 0.7 reduce.7
  13.8 0.6 reshape.22.op_ref.refs_2_
  14.3 0.0 copy-done.5
  14.3 0.0 copy-done.6
  14.4 0.6 copy_bitcast_fusion.2
  14.9 0.6 copy_bitcast_fusion.1
  15.5 0.1 reshape.23
  15.6 0.0 copy-done.1
  15.6 0.6 reshape.25.refs_11_.refs_6_
  16.3 0.0 copy-done.2
  16.3 0.6 reshape.26.refs_12_.refs_7_
  16.9 6.1 %shard_map.91 = (f32[128,512]{1,0:T(8,128)}, f32[128,512]{1,0:T(8,128)}) custom-call(s32[8]{0:T(128)} %reshape.21.cell_ref.refs_1_, s32[8]{0:T(128)} %reshape.22.op_ref.refs_2_, f32[128,6144]{1,0:T(8,128)} %states_ref.1, f32[8,128,128]{2,1,0:T(8,128)} %refs_7_.1), custom_call_target="tpu_custom_call" | custom-call | tf_op jit(solution)/shard_map/pallas_call | solution.py:319
  23.0 0.6 pad_bitcast_fusion.refs_2_
  23.6 102.3 %shard_map.92 = (f32[1024,512]{1,0:T(8,128)}, f32[1024,512]{1,0:T(8,128)}, s32[64,128]{1,0:T(8,128)}, f32[1024,512]{1,0:T(8,128)}, f32[1024,512]{1,0:T(8,128)}) custom-call(f32[128,512]{1,0:T(8,128)} %get-tuple-element.16.refs_0_, f32[128,512]{1,0:T(8,128)} %get-tuple-element.17.refs_1_, s32[8,128]{1,0:T(8,128)} %pad_bitcast_fusion.refs_2_), custom_call_target="tpu_custom_call" | custom-call | tf_op jit(solution)/shard_map/pallas_call | solution.py:499
  125.9 0.0 copy-done.3
  125.9 0.0 copy-done.4
  125.9 0.0 all-to-all-done
  125.9 0.0 copy-start
  125.9 1.7 copy-done
  127.6 57.9 %shard_map.93 = (f32[1024,768]{1,0:T(8,128)}, f32[1024,512]{1,0:T(8,128)}, f32[1024,512]{1,0:T(8,128)}, f32[1024,512]{1,0:T(8,128)}) custom-call(s32[64,128]{1,0:T(8,128)} %get-tuple-element.18.refs_0_, s32[8]{0:T(128)} %reshape.21.cell_ref.refs_1_, s32[8]{0:T(128)} %reshape.22.op_ref.refs_2_, s32[6,8]{1,0:T(8,128)} %copy-done.3, s32[6,8]{1,0:T(8,128)} %copy-done.4, ...), custom_call_target="tpu_custom_call" | custom-call | flops 21474836480 | bytes 33554432 | tf_op jit(solution)/shard_map/pallas_call | solution.py:191
  185.5 82.9 %shard_map.94 = f32[128,6144]{1,0:T(8,128)} custom-call(s32[6,8]{1,0:T(8,128)} %get-tuple-element.32.refs_0_, s32[6,8]{1,0:T(8,128)} %get-tuple-element.34.refs_1_, f32[1024,768]{1,0:T(8,128)} %get-tuple-element.23.refs_2_, f32[1024,512]{1,0:T(8,128)} %get-tuple-element.24.refs_3_, f32[1024,512]{1,0:T(8,128)} %get-tuple-element.25.refs_4_, ...), custom_call_target="tpu_custom_call" | custom-call | flops 12884901888 | bytes 33554432 | tf_op jit(solution)/shard_map/pallas_call | solution.py:278
  268.4 3.9 %copy.32 = f32[128,6144]{1,0:T(8,128)} copy(f32[128,6144]{1,0:T(8,128)} %shard_map.94) | data formatting | bytes 6291456
  (8 shorter events, 0.0 us)
Async XLA Ops:
  3.9 8.0 %copy-start.7 = (s32[2,1,4]{2,1,0:T(1,128)S(1)}, s32[2,1,4]{2,1,0:T(1,128)}, u32[]{:S(2)}) copy-start(s32[2,1,4]{2,1,0:T(1,128)} %param.12) | copy-start | bytes 100
  3.9 9.3 %copy-start.8 = (s32[2,1,4]{2,1,0:T(1,128)S(1)}, s32[2,1,4]{2,1,0:T(1,128)}, u32[]{:S(2)}) copy-start(s32[2,1,4]{2,1,0:T(1,128)} %param.13) | copy-start | bytes 100
  3.9 10.5 %copy-start.5 = (s32[2,1,6,8]{3,1,2,0:T(1,128)S(1)}, s32[2,1,6,8]{3,1,2,0:T(1,128)}, u32[]{:S(2)}) copy-start(s32[2,1,6,8]{3,1,2,0:T(1,128)} %param.15) | copy-start | bytes 1156
  3.9 10.5 %copy-start.6 = (s32[2,1,6,8]{3,1,2,0:T(1,128)S(1)}, s32[2,1,6,8]{3,1,2,0:T(1,128)}, u32[]{:S(2)}) copy-start(s32[2,1,6,8]{3,1,2,0:T(1,128)} %param.16) | copy-start | bytes 1156
  3.9 11.8 %copy-start.1 = (f32[2,2048]{1,0:T(2,128)S(1)}, f32[2,2048]{1,0:T(2,128)}, u32[]{:S(2)}) copy-start(f32[2,2048]{1,0:T(2,128)} %param.10) | copy-start | bytes 49156
  3.9 12.4 %copy-start.2 = (f32[2,2048]{1,0:T(2,128)S(1)}, f32[2,2048]{1,0:T(2,128)}, u32[]{:S(2)}) copy-start(f32[2,2048]{1,0:T(2,128)} %param.11) | copy-start | bytes 49156
  3.9 122.0 %all-to-all-start = ((f32[128,8,768]{2,0,1:T(8,128)}), f32[128,8,768]{2,0,1:T(8,128)S(1)}, u32[]{:S(2)}, u32[]{:S(2)}) async-start(f32[128,8,768]{2,0,1:T(8,128)} %bitcast.16), calls=%async_computation | async-start | bytes 6291456 | tf_op jit(solution)/shard_map/all_to_all | solution.py:526
  14.9 110.9 %copy-start.3 = (s32[6,8]{1,0:T(8,128)}, s32[6,8]{1,0:T(8,128)S(1)}, u32[]{:S(2)}) copy-start(s32[6,8]{1,0:T(8,128)S(1)} %get-tuple-element.31.refs_3_) | copy-start | bytes 580
  15.5 110.4 %copy-start.4 = (s32[6,8]{1,0:T(8,128)}, s32[6,8]{1,0:T(8,128)S(1)}, u32[]{:S(2)}) copy-start(s32[6,8]{1,0:T(8,128)S(1)} %get-tuple-element.33.refs_4_) | copy-start | bytes 580
  125.9 1.7 copy-start

commit v4 on v3

--- a/solution.py
+++ b/solution.py
@@ -335,9 +335,11 @@
 
 
 def gather_kernel(member_n, space_n, *refs):
-    ins, refs = refs[:3], refs[3:]
+    ins, states_ref, refs = refs[:3], refs[3], refs[4:]
     outs, refs = refs[:3], refs[3:]
-    prev_ref, next_ref, send_sem, recv_sem, halo_send, halo_recv, local_sem = refs
+    prev_ref, next_ref, cells_ref, send_sem, recv_sem, halo_send, halo_recv, local_sem = refs[:8]
+    swap_send, swap_recv = refs[8:]
+    share, width = states_ref.shape[0], cells_ref.shape[1]
     me = lax.axis_index("member")
     slab = lax.axis_index("space")
     line = member_n // 2
@@ -353,21 +355,30 @@
             barrier, inc=1, device_id=(member, space), device_id_type=pl.DeviceIdType.MESH
         )
 
-    greet(mate, slab)
     greet(me, after)
     greet(me, before)
-
-    @pl.when(at > 0)
-    def _():
-        greet(me - 2, slab)
-
-    @pl.when(at < line - 1)
-    def _():
-        greet(me + 2, slab)
-
-    pl.semaphore_wait(
-        barrier, 3 + jnp.where(at > 0, 1, 0) + jnp.where(at < line - 1, 1, 0)
-    )
+    for hop_by in range(1, member_n):
+        greet(lax.rem(me + hop_by, member_n), slab)
+    pl.semaphore_wait(barrier, member_n + 1)
+
+    def states_for(member):
+        return states_ref.at[:, pl.ds(pl.multiple_of(member * width, BLK), width)]
+
+    def cells_of(member):
+        return cells_ref.at[pl.ds(pl.multiple_of(member * share, 8), share)]
+
+    def swap(hop_by):
+        peer = lax.rem(me + hop_by, member_n)
+        return send(
+            states_for(peer), cells_of(me), swap_send.at[hop_by], swap_recv.at[me], peer, slab
+        )
+
+    hops = sorted(range(1, member_n), key=lambda k: (abs(k - line), k))
+    each = -(-len(hops) // line)
+
+    def swaps(step):
+        for hop_by in hops[step * each:(step + 1) * each]:
+            swap(hop_by).start()
 
     def rows(ref, item, block):
         size = ins[item].shape[0]
@@ -412,7 +423,9 @@
         pltpu.make_async_copy(ins[item], rows(outs[item], item, me), local_sem.at[item])
         for item in range(3)
     ]
-    for copy in local:
+    kept = pltpu.make_async_copy(states_for(me), cells_of(me), local_sem.at[3])
+    swaps(0)
+    for copy in local + [kept]:
         copy.start()
 
     def landed(item, block):
@@ -453,6 +466,7 @@
                 if item == 0:
                     sides(high)
 
+        swaps(step)
         if step == 1:
             from_mate(mate)
         else:
@@ -472,8 +486,14 @@
     def _():
         from_mate(mate + 2 * (line - 1))
 
-    for copy in local:
+    for copy in local + [kept]:
         copy.wait()
+    for hop_by in range(1, member_n):
+        swap(hop_by).wait_send()
+        peer = lax.rem(me + hop_by, member_n)
+        send(
+            states_for(peer), cells_of(peer), swap_send.at[hop_by], swap_recv.at[peer], peer, slab
+        ).wait_recv()
     for block in range(member_n):
         for way in range(2):
             side(block, way).wait()
@@ -492,24 +512,28 @@
                 hop(item, block, 2, mate).wait_send()
 
 
-def gather(observed, picked, ints):
+def gather(observed, picked, ints, states):
     member_n, space_n = lax.axis_size("member"), lax.axis_size("space")
     parts = (observed, picked, ints)
     out = [jax.ShapeDtypeStruct((member_n * a.shape[0], a.shape[1]), a.dtype) for a in parts]
+    share, width = states.shape
+    cells = jax.ShapeDtypeStruct((share * member_n, width // member_n), states.dtype)
     return pl.pallas_call(
         functools.partial(gather_kernel, member_n, space_n),
-        out_shape=out + [out[0], out[0]],
-        in_specs=[pl.BlockSpec(memory_space=pltpu.VMEM)] * 3,
-        out_specs=[pl.BlockSpec(memory_space=pl.ANY)] * 5,
+        out_shape=out + [out[0], out[0], cells],
+        in_specs=[pl.BlockSpec(memory_space=pltpu.VMEM)] * 3 + [pl.BlockSpec(memory_space=pl.ANY)],
+        out_specs=[pl.BlockSpec(memory_space=pl.ANY)] * 6,
         scratch_shapes=[
             pltpu.SemaphoreType.DMA((3, member_n, 3)),
             pltpu.SemaphoreType.DMA((3, member_n)),
             pltpu.SemaphoreType.DMA((member_n, 2)),
             pltpu.SemaphoreType.DMA((member_n, 2)),
-            pltpu.SemaphoreType.DMA((3,)),
+            pltpu.SemaphoreType.DMA((4,)),
+            pltpu.SemaphoreType.DMA((member_n,)),
+            pltpu.SemaphoreType.DMA((member_n,)),
         ],
         compiler_params=pltpu.CompilerParams(collective_id=0, has_side_effects=True),
-    )(*parts)
+    )(*parts, states)
 
 
 def per_device(
@@ -523,9 +547,8 @@
     extra = -(-ints.shape[0] // (8 * BLK)) * 8
     ints = jnp.pad(ints, (0, extra * BLK - ints.shape[0])).reshape(extra, BLK)
 
-    cells = lax.all_to_all(states, "member", split_axis=1, concat_axis=0, tiled=True)
     observed, picked = pick_blocks(cell, ops, states, op_table)
-    own, picked, ints, before, after = gather(observed, picked, ints)
+    own, picked, ints, before, after, cells = gather(observed, picked, ints, states)
     cells, own, before, after = first_batch(
         ints, cell, ops, loc_obs[0, 0], loc_tile[0, 0], picked, cells, op_table,
         (before, own, after), values, weights, loc_tiles,

time: 274 us -> 272 us (level)
  starting transfers between devices: 7.42 us -> 0 us
  Pallas kernels: 249 us -> 255 us
    all_to_all x1 -> x0, starting transfers between devices: 7.42 us -> none  [per_device(): lax.all_to_all(states, 'member', split_axis=1, concat_axis=0, tiled=True)]
    all_to_all x1 -> x0, local copies, waits for them, and re-layouts: 3.85 us -> none  [per_device(): lax.all_to_all(states, 'member', split_axis=1, concat_axis=0, tiled=True)]
    pallas_call x1, Pallas kernels: 82.9 us -> 86.1 us  [last_batch(): pl.pallas_call(functools.partial(last_kernel, nb, ob, loc, member_n, lax....]
    unnamed x20 -> x6, local copies, waits for them, and re-layouts: 6.08 us -> 4.37 us
  transfers between devices with their start and end apart: 1 -> 0, of which waited for: 0 -> 0; matrix products, arithmetic and copies ran while one was open for 2% -> 0% of each run, Pallas kernels for 40% -> 0%
where the time goes in v4:
time: 272 us; the launch traced here: 270 us
  Pallas kernels  255 us (94%)
  local copies, waits for them, and re-layouts  11.7 us (4%)
    pallas_call x1, Pallas kernels, gather(): pl.pallas_call(functools.partial(gather_kernel, member_n, space_n), out_s...  104 us
    pallas_call x1, Pallas kernels, last_batch(): pl.pallas_call(functools.partial(last_kernel, nb, ob, loc, member_n, lax....  86.1 us
    pallas_call x1, Pallas kernels, first_batch(): pl.pallas_call(functools.partial(first_kernel, nb, ob, loc, lax.axis_size...  58.9 us
    pallas_call x1, Pallas kernels, pick_blocks(): pl.pallas_call(functools.partial(pick_kernel, ob), grid_spec=pltpu.Prefet...  6.1 us

profile of v4, /device:TPU:0, one launch (start us, length us, event | category | flops | bytes accessed | tf_op | source)
XLA Modules:
  0.0 269.7 jit_solution(9675759638695607974)
XLA Ops:
  0.0 0.5 broadcast.8
  0.5 1.3 reduce.6
  1.9 0.7 reshape.18.cell_ref.refs_1_
  2.5 1.3 reduce.7
  3.9 0.7 reshape.19.op_ref.refs_2_
  4.5 0.7 fusion
  5.2 0.6 copy_bitcast_fusion.1
  5.8 0.0 copy-start
  5.8 0.7 fusion.1
  6.5 0.6 copy_bitcast_fusion
  7.1 0.0 copy-start.1
  7.1 0.1 reshape.20
  7.2 0.6 pad_bitcast_fusion.refs_2_
  7.8 1.3 reshape.22.refs_11_.refs_6_
  9.2 1.3 reshape.23.refs_12_.refs_7_
  10.5 6.1 %shard_map.91 = (f32[128,512]{1,0:T(8,128)}, f32[128,512]{1,0:T(8,128)}) custom-call(s32[8]{0:T(128)} %reshape.18.cell_ref.refs_1_, s32[8]{0:T(128)} %reshape.19.op_ref.refs_2_, f32[128,6144]{1,0:T(8,128)} %refs_3_.1, f32[8,128,128]{2,1,0:T(8,128)} %refs_7_.1), custom_call_target="tpu_custom_call" | custom-call | tf_op jit(solution)/shard_map/pallas_call | solution.py:319
  16.6 104.2 %shard_map.92 = (f32[1024,512]{1,0:T(8,128)}, f32[1024,512]{1,0:T(8,128)}, s32[64,128]{1,0:T(8,128)}, f32[1024,512]{1,0:T(8,128)}, f32[1024,512]{1,0:T(8,128)}, /*index=5*/f32[1024,768]{1,0:T(8,128)}) custom-call(f32[128,512]{1,0:T(8,128)} %get-tuple-element.17.refs_0_, f32[128,512]{1,0:T(8,128)} %get-tuple-element.18.refs_1_, ...), custom_call_target="tpu_custom_call" | custom-call | tf_op jit(solution)/shard_map/pallas_call | solution.py:521
  120.9 0.0 copy-done
  120.9 0.0 copy-done.1
  120.9 58.9 %shard_map.93 = (f32[1024,768]{1,0:T(8,128)}, f32[1024,512]{1,0:T(8,128)}, f32[1024,512]{1,0:T(8,128)}, f32[1024,512]{1,0:T(8,128)}) custom-call(s32[64,128]{1,0:T(8,128)} %get-tuple-element.19.refs_0_, s32[8]{0:T(128)} %reshape.18.cell_ref.refs_1_, s32[8]{0:T(128)} %reshape.19.op_ref.refs_2_, s32[6,8]{1,0:T(8,128)} %copy-done, s32[6,8]{1,0:T(8,128)} %copy-done.1, ...), custom_call_target="tpu_custom_call" | custom-call | flops 21474836480 | bytes 33554432 | tf_op jit(solution)/shard_map/pallas_call | solution.py:191
  179.8 86.1 %shard_map.94 = f32[128,6144]{1,0:T(8,128)} custom-call(s32[6,8]{1,0:T(8,128)} %get-tuple-element.34.refs_0_, s32[6,8]{1,0:T(8,128)} %get-tuple-element.36.refs_1_, f32[1024,768]{1,0:T(8,128)} %get-tuple-element.25.refs_2_, f32[1024,512]{1,0:T(8,128)} %get-tuple-element.26.refs_3_, f32[1024,512]{1,0:T(8,128)} %get-tuple-element.27.refs_4_, ...), custom_call_target="tpu_custom_call" | custom-call | flops 12884901888 | bytes 33554432 | tf_op jit(solution)/shard_map/pallas_call | solution.py:278
  265.9 3.9 %copy.27 = f32[128,6144]{1,0:T(8,128)} copy(f32[128,6144]{1,0:T(8,128)} %shard_map.94) | data formatting | bytes 6291456
  (1 shorter events, 0.0 us)
Async XLA Ops:
  5.8 115.0 %copy-start = (s32[6,8]{1,0:T(8,128)}, s32[6,8]{1,0:T(8,128)S(1)}, u32[]{:S(2)}) copy-start(s32[6,8]{1,0:T(8,128)S(1)} %get-tuple-element.33.refs_3_) | copy-start | bytes 580
  7.1 113.8 %copy-start.1 = (s32[6,8]{1,0:T(8,128)}, s32[6,8]{1,0:T(8,128)S(1)}, u32[]{:S(2)}) copy-start(s32[6,8]{1,0:T(8,128)S(1)} %get-tuple-element.35.refs_4_) | copy-start | bytes 580
